TPU v7x, 32 devices: a whole 2x2x4 slice. The times are simulated.
32 devices in a mesh: seq: 4 (over x, core), fsdp: 8 (over z, y).
Axes of the slice: x: 2, y: 2, z: 4, core: 2. Of those that a mesh axis runs over, the one named last changes fastest.
Arguments:
- hidden_in: bfloat16 [2, 8, 1536, 768], P(None, 'fsdp', 'seq'), may hold values from -6 to 6
- cotangent: bfloat16 [2, 8, 1536, 768], P(None, 'fsdp', 'seq'), may hold values from -6 to 6
- lengths: int32 [2, 8, 3], P(None, 'fsdp'), may hold values from 1 to 768, 1536 in all within a row
- slot_order: int32 [2, 8, 1536], P(None, 'fsdp'), may hold values from 0 to 1535, each once within a row
- labels: int32 [2, 8, 3], P(None, 'fsdp'), may hold values from 0 to 13
- w_qkv: bfloat16 [768, 2304], P('fsdp'), may hold values from -0.21875 to 0.21875
- bias_query: bfloat16 [768], P('fsdp'), may hold values from -1.75 to 1.75
- bias_value: bfloat16 [768], P('fsdp'), may hold values from -0.125 to 0.125
- w_out: bfloat16 [768, 768], P('fsdp'), may hold values from -3.5 to 3.5
- bias_out: bfloat16 [768], P('fsdp'), may hold values from -1.75 to 1.75
- gain_attn: bfloat16 [768], P('fsdp'), may hold values from 0.5 to 1.5
- shift_attn: bfloat16 [768], P('fsdp'), may hold values from -1.25 to 1.25
- w_up: bfloat16 [768, 3072], P('fsdp'), may hold values from -0.21875 to 0.21875
- bias_up: bfloat16 [3072], P('fsdp'), may hold values from -1.75 to 1.75
- w_down: bfloat16 [3072, 768], P('fsdp'), may hold values from -0.109375 to 0.109375
- bias_down: bfloat16 [768], P('fsdp'), may hold values from -1.75 to 1.75
- gain_ffn: bfloat16 [768], P('fsdp'), may hold values from 0.5 to 1.5
- shift_ffn: bfloat16 [768], P('fsdp'), may hold values from -1.75 to 1.75
- w_student: bfloat16 [768, 128], P('fsdp'), may hold values from -0.21875 to 0.21875
- bias_student: bfloat16 [128], P('fsdp'), may hold values from -1.75 to 1.75
- pool_query: float32 [2, 64], replicated, may hold values from -1.5 to 1.5
- w_pool: float32 [128, 128], replicated, may hold values from -1.5 to 1.5
- bias_pool: float32 [128], replicated, may hold values from -1.75 to 1.75
- w_class: float32 [128, 14], replicated, may hold values from -2 to 2
- bias_class: float32 [14], replicated, may hold values from -3 to 3
Outputs:
- hidden_out: bfloat16 [2, 8, 1536, 768], P(None, 'fsdp', 'seq')
- logits: float32 [2, 8, 3, 14], P(None, 'fsdp')
- grad_input: float32 [2, 8, 1536, 768], P(None, 'fsdp', 'seq')
- grad_w_qkv: float32 [768, 2304], P('fsdp')
- grad_bias_query: float32 [768], P('fsdp')
- grad_bias_value: float32 [768], P('fsdp')
- grad_w_out: float32 [768, 768], P('fsdp')
- grad_bias_out: float32 [768], P('fsdp')
- grad_gain_attn: float32 [768], P('fsdp')
- grad_shift_attn: float32 [768], P('fsdp')
- grad_w_up: float32 [768, 3072], P('fsdp')
- grad_bias_up: float32 [3072], P('fsdp')
- grad_w_down: float32 [3072, 768], P('fsdp')
- grad_bias_down: float32 [768], P('fsdp')
- grad_gain_ffn: float32 [768], P('fsdp')
- grad_shift_ffn: float32 [768], P('fsdp')
- grad_w_student: float32 [768, 128], P('fsdp')
- grad_bias_student: float32 [128], P('fsdp')
- grad_pool_query: float32 [2, 64], replicated
- grad_w_pool: float32 [128, 128], replicated
- grad_bias_pool: float32 [128], replicated
- grad_w_class: float32 [128, 14], replicated
- grad_bias_class: float32 [14], replicated
Inputs may be any that keep to these rules, and one draw needn't show every extreme that they name: Each row of 3 lengths sums to 1536, and its largest is exactly 768. `slot_order`: each row names every number from 0 to 1535 once.
All inputs are finite; a program needn't handle non-finite values.
Results may differ from a plain program's by a relative error of at most 0.024.
The roundings to bfloat16 on the way count: a program that leaves them out, or rounds other values in their place, can miss the bound.
Values may be sent and summed in bfloat16 or wider, within the bound.
No kernel may reach another device: no remote copies, remote signals or barrier semaphores. Data moves between devices by JAX's collectives and lax.ppermute only.
A program may use at most 192 MiB of HBM per device.

v0:
```python
import jax
import jax.numpy as jnp
from jax import lax
from jax.sharding import PartitionSpec as P

HEAD_DIM = 64


highest = lax.Precision.HIGHEST
masked_value = -1e30


def combined_all(value, axis, join):
    pieces = jax.tree.map(lambda part: lax.all_gather(part, axis), value)
    head = jax.tree.map(lambda part: part[0], pieces)
    tail = jax.tree.map(lambda part: part[1:], pieces)
    subtotal, _ = lax.scan(lambda subtotal, section: (join(subtotal, section), None), head, tail)
    return subtotal


def layer_norm(values, gain, shift):
    center = values - jnp.mean(values, axis=-1, keepdims=True)
    spread = jnp.mean(center * center, axis=-1, keepdims=True)
    return center * lax.rsqrt(spread + 1e-06) * gain + shift


def exact_gelu(values):
    return jax.nn.gelu(values, approximate=False)


def segment_ids(order_row, length_row):
    ends = jnp.cumsum(length_row)
    above = (order_row[:, None] >= ends[None, :-1]).astype(jnp.int32)
    return jnp.sum(above, axis=1)


def classify(pooled, w_pool, bias_pool, w_class, bias_class, labels):
    inner = jnp.tanh(
        jnp.dot(pooled, w_pool, precision=highest, preferred_element_type=jnp.float32) + bias_pool
    )
    logits = (
        jnp.dot(inner, w_class, precision=highest, preferred_element_type=jnp.float32) + bias_class
    )
    row_peak = jnp.max(logits, axis=-1, keepdims=True)
    log_total = row_peak[:, 0] + jnp.log(jnp.sum(jnp.exp(logits - row_peak), axis=-1))
    classes = jnp.arange(logits.shape[1])
    picked = jnp.sum(jnp.where(classes[None, :] == labels[:, None], logits, 0.0), axis=-1)
    return (jnp.sum(log_total - picked), logits)


def big_product(left, right):
    return jnp.dot(left, right, preferred_element_type=jnp.float32)


def left_product(left, right):
    return lax.dot_general(
        left, right, (((0,), (0,)), ((), ())), preferred_element_type=jnp.float32
    )


def right_product(left, right):
    return lax.dot_general(
        left, right, (((1,), (1,)), ((), ())), preferred_element_type=jnp.float32
    )


def combine_parts(first, second):
    new_peak = jnp.maximum(first[0], second[0])
    first_scale = jnp.exp(first[0] - new_peak)
    second_scale = jnp.exp(second[0] - new_peak)
    return (
        new_peak,
        first[1] * first_scale + second[1] * second_scale,
        first[2] * first_scale[:, :, None] + second[2] * second_scale[:, :, None],
    )


def fetch_forward(shards):
    return (
        lax.all_gather(shards[0], "fsdp", axis=0, tiled=True),
        lax.all_gather(shards[1], "fsdp", axis=0, tiled=True),
        lax.all_gather(shards[2], "fsdp", axis=0, tiled=True),
        lax.all_gather(shards[3], "fsdp", axis=0, tiled=True),
        lax.all_gather(shards[4], "fsdp", axis=0, tiled=True),
        lax.all_gather(shards[5], "fsdp", axis=0, tiled=True),
        lax.all_gather(shards[6], "fsdp", axis=0, tiled=True),
        lax.all_gather(shards[7], "fsdp", axis=0, tiled=True),
        lax.all_gather(shards[8], "fsdp", axis=0, tiled=True),
        lax.all_gather(shards[9], "fsdp", axis=0, tiled=True),
        lax.all_gather(shards[10], "fsdp", axis=0, tiled=True),
        lax.all_gather(shards[11], "fsdp", axis=0, tiled=True),
        lax.all_gather(shards[12], "fsdp", axis=0, tiled=True),
        lax.all_gather(shards[13], "fsdp", axis=0, tiled=True),
        lax.all_gather(shards[14], "fsdp", axis=0, tiled=True),
    )


def fetch_backward(shards):
    return (
        lax.all_gather(shards[0], "fsdp", axis=0, tiled=True),
        lax.all_gather(shards[1], "fsdp", axis=0, tiled=True),
        lax.all_gather(shards[2], "fsdp", axis=0, tiled=True),
        lax.all_gather(shards[3], "fsdp", axis=0, tiled=True),
        lax.all_gather(shards[4], "fsdp", axis=0, tiled=True),
        lax.all_gather(shards[5], "fsdp", axis=0, tiled=True),
        lax.all_gather(shards[6], "fsdp", axis=0, tiled=True),
        lax.all_gather(shards[7], "fsdp", axis=0, tiled=True),
        lax.all_gather(shards[8], "fsdp", axis=0, tiled=True),
        lax.all_gather(shards[9], "fsdp", axis=0, tiled=True),
        lax.all_gather(shards[10], "fsdp", axis=0, tiled=True),
        lax.all_gather(shards[11], "fsdp", axis=0, tiled=True),
        lax.all_gather(shards[12], "fsdp", axis=0, tiled=True),
        lax.all_gather(shards[13], "fsdp", axis=0, tiled=True),
        lax.all_gather(shards[14], "fsdp", axis=0, tiled=True),
    )


def reduce_grads(full_grads):
    owned = (
        lax.psum_scatter(full_grads[0], "fsdp", scatter_dimension=0, tiled=True),
        lax.psum_scatter(full_grads[1], "fsdp", scatter_dimension=0, tiled=True),
        lax.psum_scatter(full_grads[2], "fsdp", scatter_dimension=0, tiled=True),
        lax.psum_scatter(full_grads[3], "fsdp", scatter_dimension=0, tiled=True),
        lax.psum_scatter(full_grads[4], "fsdp", scatter_dimension=0, tiled=True),
        lax.psum_scatter(full_grads[5], "fsdp", scatter_dimension=0, tiled=True),
        lax.psum_scatter(full_grads[6], "fsdp", scatter_dimension=0, tiled=True),
        lax.psum_scatter(full_grads[7], "fsdp", scatter_dimension=0, tiled=True),
        lax.psum_scatter(full_grads[8], "fsdp", scatter_dimension=0, tiled=True),
        lax.psum_scatter(full_grads[9], "fsdp", scatter_dimension=0, tiled=True),
        lax.psum_scatter(full_grads[10], "fsdp", scatter_dimension=0, tiled=True),
        lax.psum_scatter(full_grads[11], "fsdp", scatter_dimension=0, tiled=True),
        lax.psum_scatter(full_grads[12], "fsdp", scatter_dimension=0, tiled=True),
        lax.psum_scatter(full_grads[13], "fsdp", scatter_dimension=0, tiled=True),
        lax.psum_scatter(full_grads[14], "fsdp", scatter_dimension=0, tiled=True),
    )
    return (
        lax.psum(owned[0].astype(jnp.bfloat16), "seq").astype(jnp.float32),
        lax.psum(owned[1].astype(jnp.bfloat16), "seq").astype(jnp.float32),
        lax.psum(owned[2].astype(jnp.bfloat16), "seq").astype(jnp.float32),
        lax.psum(owned[3].astype(jnp.bfloat16), "seq").astype(jnp.float32),
        lax.psum(owned[4].astype(jnp.bfloat16), "seq").astype(jnp.float32),
        lax.psum(owned[5].astype(jnp.bfloat16), "seq").astype(jnp.float32),
        lax.psum(owned[6].astype(jnp.bfloat16), "seq").astype(jnp.float32),
        lax.psum(owned[7].astype(jnp.bfloat16), "seq").astype(jnp.float32),
        lax.psum(owned[8].astype(jnp.bfloat16), "seq").astype(jnp.float32),
        lax.psum(owned[9].astype(jnp.bfloat16), "seq").astype(jnp.float32),
        lax.psum(owned[10].astype(jnp.bfloat16), "seq").astype(jnp.float32),
        lax.psum(owned[11].astype(jnp.bfloat16), "seq").astype(jnp.float32),
        lax.psum(owned[12].astype(jnp.bfloat16), "seq").astype(jnp.float32),
        lax.psum(owned[13].astype(jnp.bfloat16), "seq").astype(jnp.float32),
        lax.psum(owned[14].astype(jnp.bfloat16), "seq").astype(jnp.float32),
    )


def add_tuples(first, second):
    if first is None:
        return tuple(second)
    return tuple((left + right for left, right in zip(first, second)))


def body(
    hidden_in,
    cotangent,
    lengths,
    slot_order,
    labels,
    w_qkv,
    bias_query,
    bias_value,
    w_out,
    bias_out,
    gain_attn,
    shift_attn,
    w_up,
    bias_up,
    w_down,
    bias_down,
    gain_ffn,
    shift_ffn,
    w_student,
    bias_student,
    pool_query,
    w_pool,
    bias_pool,
    w_class,
    bias_class,
):
    shards = (
        w_qkv,
        bias_query,
        bias_value,
        w_out,
        bias_out,
        gain_attn,
        shift_attn,
        w_up,
        bias_up,
        w_down,
        bias_down,
        gain_ffn,
        shift_ffn,
        w_student,
        bias_student,
    )
    seq_count = lax.axis_size("seq")
    seq_index = lax.axis_index("seq")
    micro_count = hidden_in.shape[0]
    local_tokens = hidden_in.shape[2]
    model_width = hidden_in.shape[3]
    group_tokens = slot_order.shape[2]
    seq_total = lengths.shape[2]
    pool_heads = pool_query.shape[0]
    head_dim = HEAD_DIM
    head_width = model_width // seq_count
    local_heads = head_width // head_dim
    scaling = head_dim ** (-0.5)
    block_rows = min(512, group_tokens)
    blocks = group_tokens // block_rows
    first_seq = (seq_index == 0).astype(jnp.float32)

    def split_blocks(values):
        return values.reshape(blocks, block_rows, local_heads, head_dim)

    def masked_scores(query_part, key_all, segment_part, segments):
        scores = (
            jnp.einsum("qhd,khd->hqk", query_part, key_all, preferred_element_type=jnp.float32)
            * scaling
        )
        same_doc = (segment_part[:, None] == segments[None, :])[None]
        return jnp.where(same_doc, scores, masked_value)

    outputs = []
    logit_list = []
    grad_inputs = []
    owned_total = None
    head_total = None
    for micro_index in range(micro_count):
        weights = fetch_forward(shards)
        (
            full_qkv,
            full_query_bias,
            full_value_bias,
            full_out,
            full_out_bias,
            full_gain_attn,
            full_shift_attn,
            full_up,
            full_up_bias,
            full_down,
            full_down_bias,
            full_gain_ffn,
            full_shift_ffn,
            full_student,
            full_student_bias,
        ) = weights
        hidden = hidden_in[micro_index, 0]
        label_row = labels[micro_index, 0]
        segments = segment_ids(slot_order[micro_index, 0], lengths[micro_index, 0])
        segment_local = lax.dynamic_slice_in_dim(segments, seq_index * local_tokens, local_tokens)
        projected = big_product(hidden, full_qkv)
        query = (projected[:, :model_width] + full_query_bias.astype(jnp.float32)).astype(
            jnp.bfloat16
        )
        key_rows = projected[:, model_width : 2 * model_width].astype(jnp.bfloat16)
        value_rows = (projected[:, 2 * model_width :] + full_value_bias.astype(jnp.float32)).astype(
            jnp.bfloat16
        )
        query_all, key_all, value_all = (
            lax.all_to_all(
                query.reshape(local_tokens, seq_count, head_width),
                "seq",
                split_axis=1,
                concat_axis=0,
                tiled=True,
            ),
            lax.all_to_all(
                key_rows.reshape(local_tokens, seq_count, head_width),
                "seq",
                split_axis=1,
                concat_axis=0,
                tiled=True,
            ),
            lax.all_to_all(
                value_rows.reshape(local_tokens, seq_count, head_width),
                "seq",
                split_axis=1,
                concat_axis=0,
                tiled=True,
            ),
        )
        query_all = query_all.reshape(group_tokens, local_heads, head_dim)
        key_all = key_all.reshape(group_tokens, local_heads, head_dim)
        value_all = value_all.reshape(group_tokens, local_heads, head_dim)

        def forward_block(inputs):
            query_part, segment_part = inputs
            scores = masked_scores(query_part, key_all, segment_part, segments)
            row_peak = jnp.max(scores, axis=-1, keepdims=True)
            exponent = jnp.exp(scores - row_peak)
            totals = jnp.sum(exponent, axis=-1, keepdims=True)
            probs = (exponent / totals).astype(jnp.bfloat16)
            context = jnp.einsum(
                "hqk,khd->qhd", probs, value_all, preferred_element_type=jnp.float32
            )
            return (context.astype(jnp.bfloat16), row_peak[:, :, 0] + jnp.log(totals[:, :, 0]))

        contexts, attend_log_totals = lax.map(
            forward_block, (split_blocks(query_all), segments.reshape(blocks, block_rows))
        )
        context_heads = contexts.reshape(group_tokens, 1, head_width)
        context = lax.all_to_all(
            context_heads, "seq", split_axis=0, concat_axis=1, tiled=True
        ).reshape(local_tokens, model_width)
        branch = big_product(context, full_out) + full_out_bias.astype(jnp.float32)
        normed, first_norm_back = jax.vjp(
            layer_norm,
            hidden.astype(jnp.float32) + branch,
            full_gain_attn.astype(jnp.float32),
            full_shift_attn.astype(jnp.float32),
        )
        normed_low = normed.astype(jnp.bfloat16)
        upward = big_product(normed_low, full_up) + full_up_bias.astype(jnp.float32)
        active, gelu_back = jax.vjp(exact_gelu, upward)
        active_low = active.astype(jnp.bfloat16)
        downward = big_product(active_low, full_down) + full_down_bias.astype(jnp.float32)
        final, second_norm_back = jax.vjp(
            layer_norm,
            normed + downward,
            full_gain_ffn.astype(jnp.float32),
            full_shift_ffn.astype(jnp.float32),
        )
        final_low = final.astype(jnp.bfloat16)
        outputs.append(final_low)
        student = big_product(final_low, full_student) + full_student_bias.astype(jnp.float32)
        pieces = student.reshape(local_tokens, pool_heads, -1)
        energy = jnp.sum(pieces * pool_query[None], axis=-1)
        members = (segment_local[:, None] == jnp.arange(seq_total, dtype=jnp.int32)[None, :])[
            :, :, None
        ]
        local_peak = jnp.max(jnp.where(members, energy[:, None, :], masked_value), axis=0)
        local_weights = jnp.exp(
            jnp.where(members, energy[:, None, :] - local_peak[None], masked_value)
        )
        local_total = jnp.sum(local_weights, axis=0)
        local_accum = jnp.einsum("tnh,thd->nhd", local_weights, pieces, precision=highest)
        global_peak, global_total, global_accum = combined_all(
            (local_peak, local_total, local_accum), "seq", combine_parts
        )
        pooled_heads = global_accum / global_total[:, :, None]
        pooled = pooled_heads.reshape(seq_total, -1)

        def head_loss(pooled_rows, pool_weight, pool_bias, class_weight, class_bias):
            return classify(
                pooled_rows, pool_weight, pool_bias, class_weight, class_bias, label_row
            )

        loss_value, head_back, logit_rows = jax.vjp(
            head_loss, pooled, w_pool, bias_pool, w_class, bias_class, has_aux=True
        )
        logit_list.append(logit_rows)
        grad_pooled, grad_wpool, grad_bpool, grad_wclass, grad_bclass = head_back(
            jnp.ones_like(loss_value)
        )
        weights = fetch_backward(shards)
        (
            full_qkv,
            full_query_bias,
            full_value_bias,
            full_out,
            full_out_bias,
            full_gain_attn,
            full_shift_attn,
            full_up,
            full_up_bias,
            full_down,
            full_down_bias,
            full_gain_ffn,
            full_shift_ffn,
            full_student,
            full_student_bias,
        ) = weights
        alpha = (
            jnp.exp(jnp.where(members, energy[:, None, :] - global_peak[None], masked_value))
            / global_total[None]
        )
        grad_heads = grad_pooled.reshape(seq_total, pool_heads, -1)
        along = jnp.einsum("thd,nhd->tnh", pieces, grad_heads, precision=highest)
        baseline = jnp.sum(pooled_heads * grad_heads, axis=-1)
        grad_energy = jnp.sum(alpha * (along - baseline[None]), axis=1)
        grad_pieces = (
            jnp.einsum("tnh,nhd->thd", alpha, grad_heads, precision=highest)
            + grad_energy[:, :, None] * pool_query[None]
        )
        grad_pool_query = jnp.einsum("th,thd->hd", grad_energy, pieces, precision=highest)
        grad_student = grad_pieces.reshape(local_tokens, -1).astype(jnp.bfloat16)
        grad_w_student = left_product(final_low, grad_student)
        grad_bias_student = jnp.sum(grad_student.astype(jnp.float32), axis=0)
        grad_final = cotangent[micro_index, 0].astype(jnp.float32) + right_product(
            grad_student, full_student
        )
        grad_mid, grad_gain_ffn, grad_shift_ffn = second_norm_back(grad_final)
        grad_down = grad_mid.astype(jnp.bfloat16)
        grad_bias_down = jnp.sum(grad_down.astype(jnp.float32), axis=0)
        grad_w_down = left_product(active_low, grad_down)
        (grad_upward,) = gelu_back(right_product(grad_down, full_down))
        grad_up = grad_upward.astype(jnp.bfloat16)
        grad_bias_up = jnp.sum(grad_up.astype(jnp.float32), axis=0)
        grad_w_up = left_product(normed_low, grad_up)
        grad_normed = grad_mid + right_product(grad_up, full_up)
        grad_res, grad_gain_attn, grad_shift_attn = first_norm_back(grad_normed)
        grad_branch = grad_res.astype(jnp.bfloat16)
        grad_bias_out = jnp.sum(grad_branch.astype(jnp.float32), axis=0)
        grad_w_out = left_product(context, grad_branch)
        grad_context = right_product(grad_branch, full_out).astype(jnp.bfloat16)
        grad_context_all = lax.all_to_all(
            grad_context.reshape(local_tokens, seq_count, head_width),
            "seq",
            split_axis=1,
            concat_axis=0,
            tiled=True,
        )
        grad_context_all = grad_context_all.reshape(group_tokens, local_heads, head_dim)

        def backward_block(carry, inputs):
            query_part, segment_part, log_part, grad_part = inputs
            scores = masked_scores(query_part, key_all, segment_part, segments)
            soft = jnp.exp(scores - log_part[:, :, None])
            grad_soft = jnp.einsum(
                "qhd,khd->hqk", grad_part, value_all, preferred_element_type=jnp.float32
            )
            inner = jnp.sum(soft * grad_soft, axis=-1, keepdims=True)
            grad_scores = (soft * (grad_soft - inner)).astype(jnp.bfloat16)
            grad_query = (
                jnp.einsum("hqk,khd->qhd", grad_scores, key_all, preferred_element_type=jnp.float32)
                * scaling
            )
            grad_key = (
                carry[0]
                + jnp.einsum(
                    "hqk,qhd->khd", grad_scores, query_part, preferred_element_type=jnp.float32
                )
                * scaling
            )
            grad_value = carry[1] + jnp.einsum(
                "hqk,qhd->khd",
                soft.astype(jnp.bfloat16),
                grad_part,
                preferred_element_type=jnp.float32,
            )
            return ((grad_key, grad_value), grad_query.astype(jnp.bfloat16))

        zeros = jnp.zeros((group_tokens, local_heads, head_dim), jnp.float32)
        (grad_key, grad_value), grad_query = lax.scan(
            backward_block,
            (zeros, zeros),
            (
                split_blocks(query_all),
                segments.reshape(blocks, block_rows),
                attend_log_totals,
                split_blocks(grad_context_all),
            ),
        )
        heads_query = grad_query.reshape(group_tokens, 1, head_width)
        heads_key = grad_key.astype(jnp.bfloat16).reshape(group_tokens, 1, head_width)
        heads_value = grad_value.astype(jnp.bfloat16).reshape(group_tokens, 1, head_width)
        back_query, back_key, back_value = (
            lax.all_to_all(heads_query, "seq", split_axis=0, concat_axis=1, tiled=True),
            lax.all_to_all(heads_key, "seq", split_axis=0, concat_axis=1, tiled=True),
            lax.all_to_all(heads_value, "seq", split_axis=0, concat_axis=1, tiled=True),
        )
        back_query = back_query.reshape(local_tokens, model_width)
        back_key = back_key.reshape(local_tokens, model_width)
        back_value = back_value.reshape(local_tokens, model_width)
        grad_proj = jnp.concatenate([back_query, back_key, back_value], axis=1)
        grad_bias_query = jnp.sum(back_query.astype(jnp.float32), axis=0)
        grad_bias_value = jnp.sum(back_value.astype(jnp.float32), axis=0)
        grad_w_qkv = left_product(hidden, grad_proj)
        grad_inputs.append(grad_res + right_product(grad_proj, full_qkv))
        full_grads = (
            grad_w_qkv,
            grad_bias_query,
            grad_bias_value,
            grad_w_out,
            grad_bias_out,
            grad_gain_attn,
            grad_shift_attn,
            grad_w_up,
            grad_bias_up,
            grad_w_down,
            grad_bias_down,
            grad_gain_ffn,
            grad_shift_ffn,
            grad_w_student,
            grad_bias_student,
        )
        owned_total = add_tuples(owned_total, reduce_grads(full_grads))
        head_total = add_tuples(
            head_total,
            (
                grad_pool_query,
                grad_wpool * first_seq,
                grad_bpool * first_seq,
                grad_wclass * first_seq,
                grad_bclass * first_seq,
            ),
        )
    head_sums = lax.psum(head_total, ("seq", "fsdp"))
    return (
        (
            jnp.stack(outputs)[:, None],
            jnp.stack(logit_list)[:, None],
            jnp.stack(grad_inputs)[:, None],
        )
        + tuple(owned_total)
        + tuple(head_sums)
    )


def solution(mesh):
    placed = (
        P(None, "fsdp", "seq", None),
        P(None, "fsdp", "seq", None),
        P(None, "fsdp", None),
        P(None, "fsdp", None),
        P(None, "fsdp", None),
        P("fsdp", None),
        P("fsdp"),
        P("fsdp"),
        P("fsdp", None),
        P("fsdp"),
        P("fsdp"),
        P("fsdp"),
        P("fsdp", None),
        P("fsdp"),
        P("fsdp", None),
        P("fsdp"),
        P("fsdp"),
        P("fsdp"),
        P("fsdp", None),
        P("fsdp"),
        P(),
        P(),
        P(),
        P(),
        P(),
    )
    return jax.shard_map(
        body,
        mesh=mesh,
        in_specs=placed,
        out_specs=(
            P(None, "fsdp", "seq", None),
            P(None, "fsdp", None, None),
            P(None, "fsdp", "seq", None),
            P("fsdp", None),
            P("fsdp"),
            P("fsdp"),
            P("fsdp", None),
            P("fsdp"),
            P("fsdp"),
            P("fsdp"),
            P("fsdp", None),
            P("fsdp"),
            P("fsdp", None),
            P("fsdp"),
            P("fsdp"),
            P("fsdp"),
            P("fsdp", None),
            P("fsdp"),
            P(),
            P(),
            P(),
            P(),
            P(),
        ),
        check_vma=False,
    )
```

profile of v0, /device:TPU:8, one launch (start us, length us, event | category | flops | bytes accessed | tf_op | source)
XLA Modules:
  0.0 2030.3 jit_solution(12504314871200741261)
XLA Ops:
  19.6 35.5 %all-reduce.31 = (bf16[768]{0:T(1024)(128)(2,1)S(1)}, bf16[768]{0:T(1024)(128)(2,1)S(1)}, bf16[768]{0:T(1024)(128)(2,1)S(1)}, bf16[768]{0:T(1024)(128)(2,1)S(1)}...) all-reduce(bf16[768]{0:T(1024)(128)(2,1)S(1)} %dynamic-update-slice, ...), channel_id=1, replica_groups=mesh['seq'=4,'fsdp'=8] {'fsdp'}, use_global_device_ids=true, to_apply=%add | all-reduce | flops 6272 | bytes 25088
  55.1 21.5 %all-gather.16.cloned.1.call-done = bf16[768,2304]{1,0:T(8,128)(2,1)} async-done(((bf16[96,2304]{1,0:T(8,128)(2,1)}), bf16[768,2304]{1,0:T(8,128)(2,1)}) %all-gather.16.cloned.1.call-update) | async-done | bytes 3538960 | tf_op jit(solution)/shard_map/all_gather | solution.py:80
  144.2 25.5 %all-gather.6 = bf16[8,1,384]{2,1,0:T(2,128)(2,1)S(1)} all-gather(bf16[1,1,384]{2,1,0:T(2,128)(2,1)S(1)} %reshape.684), channel_id=1, replica_groups=mesh['seq'=4,'fsdp'=8] {'fsdp'}, dimensions={0}, use_global_device_ids=true | all-gather | bytes 6912 | tf_op jit(solution)/shard_map/all_gather | solution.py:88
  172.7 32.1 %all_gather.119 = bf16[768,128]{1,0:T(8,128)(2,1)} all-gather(bf16[96,128]{1,0:T(8,128)(2,1)S(1)} %copy-done.106), channel_id=1, replica_groups=mesh['seq'=4,'fsdp'=8] {'fsdp'}, dimensions={0}, use_global_device_ids=true | all-gather | bytes 221184 | tf_op jit(solution)/shard_map/all_gather | solution.py:93
  215.8 26.9 %while.83 = (s32[]{:T(128)}, bf16[3,512,3,64]{1,3,2,0:T(8,128)(2,1)S(1)}, f32[3,3,512]{2,1,0:T(4,128)S(1)}, s32[3,512]{1,0:T(4,128)S(1)}, s32[1536]{0:T(1024)S(1...) while((s32[]{:T(128)}, ...), condition=%wide.region_15.16_spmd, body=%wide.region_12.15_spmd.sunk | while | flops 633174528 | bytes 33101932 | solution.py:307
  271.0 26.9 %while.82 = (s32[]{:T(128)}, bf16[3,512,3,64]{1,3,2,0:T(8,128)(2,1)S(1)}, f32[3,3,512]{2,1,0:T(4,128)S(1)}, s32[3,512]{1,0:T(4,128)S(1)}, s32[1536]{0:T(1024)S(1...) while((s32[]{:T(128)}, ...), condition=%wide.region_5.6_spmd, body=%wide.region_2.5_spmd.sunk | while | flops 633174528 | bytes 33101932 | solution.py:307
  337.1 15.4 multiply_convert_fusion.2
  358.5 14.9 multiply_convert_fusion.3
  496.6 97.3 %while.86 = (s32[]{:T(128)}, f32[1536,3,64]{0,2,1:T(8,128)S(1)}, f32[1536,3,64]{0,2,1:T(8,128)S(1)}, bf16[3,512,3,64]{1,3,2,0:T(8,128)(2,1)}, bf16[3,512,3,64]{1...) while((s32[]{:T(128)}, f32[1536,3,64]{0,2,1:T(8,128)S(1)}, ...), condition=%wide.region_42.43_spmd.clone, body=%wide.region_40.42_spmd.clone.sunk | while | flops 1533639168 | bytes 155366096 | solution.py:453
  604.6 10.8 reduce.21
  704.7 97.6 %while.87 = (s32[]{:T(128)}, f32[1536,3,64]{0,2,1:T(8,128)S(1)}, f32[1536,3,64]{0,2,1:T(8,128)S(1)}, bf16[3,512,3,64]{1,3,2,0:T(8,128)(2,1)}, bf16[3,512,3,64]{1...) while((s32[]{:T(128)}, f32[1536,3,64]{0,2,1:T(8,128)S(1)}, ...), condition=%wide.region_55.56_spmd.clone, body=%wide.region_53.55_spmd.clone.sunk | while | flops 1533639168 | bytes 155366096 | solution.py:453
  812.8 10.8 reduce.18
  935.7 87.7 %reduce-scatter.33.cloned.1.call-done = f32[96,2304]{1,0:T(8,128)} async-done(((f32[768,2304]{1,0:T(8,128)}), f32[96,2304]{1,0:T(8,128)}) %reduce-scatter.33.cloned.1.call-update) | async-done | bytes 884752
  1025.6 162.2 %reduce-scatter.21.cloned.1.call-done = f32[96,3072]{1,0:T(8,128)} async-done(((f32[768,3072]{1,0:T(8,128)}), f32[96,3072]{1,0:T(8,128)}) %reduce-scatter.21.cloned.1.call-update) | async-done | bytes 1179664 | tf_op jit(solution)/shard_map/reduce_scatter | solution.py:127
  1190.0 162.5 %reduce-scatter.19.cloned.1.call-done = f32[96,3072]{1,0:T(8,128)} async-done(((f32[768,3072]{1,0:T(8,128)}), f32[96,3072]{1,0:T(8,128)}) %reduce-scatter.19.cloned.1.call-update) | async-done | bytes 1179664 | tf_op jit(solution)/shard_map/reduce_scatter | solution.py:127
  1354.7 162.7 %reduce-scatter.25.cloned.1.call-done = f32[384,768]{1,0:T(8,128)} async-done(((f32[3072,768]{1,0:T(8,128)}), f32[384,768]{1,0:T(8,128)}) %reduce-scatter.25.cloned.1.call-update) | async-done | bytes 1179664 | tf_op jit(solution)/shard_map/reduce_scatter | solution.py:129
  1519.6 162.5 %reduce-scatter.23.cloned.1.call-done = f32[384,768]{1,0:T(8,128)} async-done(((f32[3072,768]{1,0:T(8,128)}), f32[384,768]{1,0:T(8,128)}) %reduce-scatter.23.cloned.1.call-update) | async-done | bytes 1179664 | tf_op jit(solution)/shard_map/reduce_scatter | solution.py:129
  1691.1 40.5 %all-reduce.29 = (f32[2,64]{1,0:T(2,128)}, f32[128]{0:T(128)}, f32[128,14]{0,1:T(8,128)}, f32[14]{0:T(128)}) all-reduce(f32[2,64]{1,0:T(2,128)S(1)} %add.548, f32[128]{0:T(128)S(1)} %add_multiply_fusion.1, f32[128,14]{0,1:T(8,128)S(1)} %fusion.113, f32[14]{0:T(128)S(1)} %add_multiply_fusion), channel_id=1, replica_groups=mesh['seq'=4,'fsdp'=8] {'seq','fsdp'}, use_global_device_ids=true, to_apply=%region_136.137 | all-reduce | flops 2062 | bytes 16496 | tf_op jit(solution)/shard_map/psum | solution.py:507
  1731.6 16.2 reduce-scatter.27.cloned.1.call-done
  1748.6 64.1 %reduce-scatter.29.cloned.1.call-done = f32[96,128]{1,0:T(8,128)} async-done(((f32[768,128]{1,0:T(8,128)}), f32[96,128]{1,0:T(8,128)}) %reduce-scatter.29.cloned.1.call-update) | async-done | bytes 49168 | tf_op jit(solution)/shard_map/reduce_scatter | solution.py:133
  1816.7 33.9 %all-reduce.30 = (bf16[768]{0:T(1024)(128)(2,1)S(1)}, bf16[768]{0:T(1024)(128)(2,1)S(1)}, bf16[768]{0:T(1024)(128)(2,1)S(1)}, bf16[768]{0:T(1024)(128)(2,1)S(1)}...) all-reduce(f32[768]{0:T(1024)S(1)} %reduce_sum.675, ...), channel_id=11, replica_groups=mesh['seq'=4,'fsdp'=8] {'fsdp'}, use_global_device_ids=true, to_apply=%region_64.65.clone | all-reduce | flops 18688 | bytes 112128
  1852.0 11.1 all-reduce.32
  1876.7 18.2 all-reduce.39.cloned.1.call-done
  1900.8 121.1 %all-reduce.37.cloned.1.call-done = f32[128,128]{1,0:T(8,128)} async-done(((f32[128,128]{1,0:T(8,128)}), f32[128,128]{1,0:T(8,128)}) %all-reduce.37.cloned.1.call-update) | async-done | bytes 65552 | tf_op jit(solution)/shard_map/psum | solution.py:507
  (913 shorter events, 803.4 us)
Async XLA Ops:
  7.2 69.4 %all-gather.16.cloned.1.call-start = ((), (), s32[]{:S(2)}) async-start(), calls=%async_computation.26 | async-start | bytes 3981312 | tf_op jit(solution)/shard_map/all_gather | solution.py:80
  7.9 325.3 %all-gather.18.cloned.1.call-start = ((), (), s32[]{:S(2)}) async-start(), calls=%async_computation.27 | async-start | bytes 1327104 | tf_op jit(solution)/shard_map/all_gather | solution.py:83
  8.7 328.4 %all-gather.20.cloned.1.call-start = ((), (), s32[]{:S(2)}) async-start(), calls=%async_computation.28 | async-start | bytes 5308416 | tf_op jit(solution)/shard_map/all_gather | solution.py:87
  114.7 237.8 %all-gather.22.cloned.1.call-start = ((), (), s32[]{:S(2)}) async-start(), calls=%async_computation.29 | async-start | bytes 5308416 | tf_op jit(solution)/shard_map/all_gather | solution.py:89
  138.0 73.3 %all-to-all-start.2 = ((bf16[384,4,192]{0,2,1:T(8,128)(2,1)}), bf16[384,4,192]{0,2,1:T(8,128)(2,1)S(1)}, u32[]{:S(2)}, u32[]{:S(2)}) async-start(bf16[384,4,192]{0,2,1:T(8,128)(2,1)} %bitcast.26), calls=%async_computation.2 | async-start | bytes 1179648 | tf_op jit(solution)/shard_map/all_to_all | solution.py:283
  211.3 53.3 %all-to-all-start.1 = ((bf16[384,4,192]{0,2,1:T(8,128)(2,1)}), bf16[384,4,192]{0,2,1:T(8,128)(2,1)}, u32[]{:S(2)}, u32[]{:S(2)}) async-start(bf16[384,4,192]{0,2,1:T(8,128)(2,1)} %bitcast.23), calls=%async_computation.1 | async-start | bytes 1179648 | tf_op jit(solution)/shard_map/all_to_all | solution.py:276
  264.6 52.6 %all-to-all-start.7 = ((bf16[4,2,36864]{2,1,0:T(2,128)(2,1)}), bf16[4,2,36864]{2,1,0:T(2,128)(2,1)}, u32[]{:S(2)}, u32[]{:S(2)}) async-start(bf16[4,2,36864]{2,1,0:T(2,128)(2,1)} %reshape.759), calls=%async_computation.7 | async-start | bytes 1179648 | tf_op jit(solution)/shard_map/all_to_all | solution.py:311
  320.7 609.4 %reduce-scatter.15.cloned.1.call-start = ((), (), s32[]{:S(2)}) async-start(), calls=%async_computation.30 | async-start | bytes 2654208 | tf_op jit(solution)/shard_map/reduce_scatter | solution.py:123
  468.7 15.5 all-to-all-start.8
  472.9 458.9 %reduce-scatter.17.cloned.1.call-start = ((), (), s32[]{:S(2)}) async-start(), calls=%async_computation.31 | async-start | bytes 2654208 | tf_op jit(solution)/shard_map/reduce_scatter | solution.py:123
  484.2 134.4 %all-to-all-start.12 = ((bf16[384,4,192]{0,2,1:T(8,128)(2,1)}), bf16[384,4,192]{0,2,1:T(8,128)(2,1)}, u32[]{:S(2)}, u32[]{:S(2)}) async-start(bf16[384,4,192]{0,2,1:T(8,128)(2,1)} %bitcast.537), calls=%async_computation.12 | async-start | bytes 1179648 | tf_op jit(solution)/shard_map/all_to_all | solution.py:415
  645.3 31.0 %all-to-all-start.10 = ((bf16[4,2,36864]{2,1,0:T(2,128)(2,1)}), bf16[4,2,36864]{2,1,0:T(2,128)(2,1)}, u32[]{:S(2)}, u32[]{:S(2)}) async-start(bf16[4,2,36864]{2,1,0:T(2,128)(2,1)} %reshape.771), calls=%async_computation.10 | async-start | bytes 1179648 | tf_op jit(solution)/shard_map/all_to_all | solution.py:468
  649.5 283.9 %reduce-scatter.31.cloned.1.call-start = ((), (), s32[]{:S(2)}) async-start(), calls=%async_computation.39 | async-start | bytes 7962624
  826.7 14.0 all-to-all-start.13
  853.7 17.4 all-to-all-start.14
  857.9 165.5 %reduce-scatter.33.cloned.1.call-start = ((), (), s32[]{:S(2)}) async-start(), calls=%async_computation.40 | async-start | bytes 7962624
  893.9 293.9 %reduce-scatter.21.cloned.1.call-start = ((), (), s32[]{:S(2)}) async-start(), calls=%async_computation.33 | async-start | bytes 10616832 | tf_op jit(solution)/shard_map/reduce_scatter | solution.py:127
  902.1 450.4 %reduce-scatter.19.cloned.1.call-start = ((), (), s32[]{:S(2)}) async-start(), calls=%async_computation.32 | async-start | bytes 10616832 | tf_op jit(solution)/shard_map/reduce_scatter | solution.py:127
  910.6 606.8 %reduce-scatter.25.cloned.1.call-start = ((), (), s32[]{:S(2)}) async-start(), calls=%async_computation.35 | async-start | bytes 10616832 | tf_op jit(solution)/shard_map/reduce_scatter | solution.py:129
  918.7 763.4 %reduce-scatter.23.cloned.1.call-start = ((), (), s32[]{:S(2)}) async-start(), calls=%async_computation.34 | async-start | bytes 10616832 | tf_op jit(solution)/shard_map/reduce_scatter | solution.py:129
  926.6 821.2 %reduce-scatter.27.cloned.1.call-start = ((), (), s32[]{:S(2)}) async-start(), calls=%async_computation.36 | async-start | bytes 442368 | tf_op jit(solution)/shard_map/reduce_scatter | solution.py:133
  928.8 883.9 %reduce-scatter.29.cloned.1.call-start = ((), (), s32[]{:S(2)}) async-start(), calls=%async_computation.37 | async-start | bytes 442368 | tf_op jit(solution)/shard_map/reduce_scatter | solution.py:133
  930.0 964.9 %all-reduce.39.cloned.1.call-start = ((), (), s32[]{:S(2)}) async-start(), calls=%async_computation.41 | async-start | bytes 7667712 | tf_op jit(solution)/shard_map/psum | solution.py:137
  1684.5 337.4 %all-reduce.37.cloned.1.call-start = ((), (), s32[]{:S(2)}) async-start(), calls=%async_computation.38 | async-start | bytes 131072 | tf_op jit(solution)/shard_map/psum | solution.py:507
  (200 other events, 4589.1 us)
Sparse Core Ops, SparseCore 0:
  10.2 66.3 all-gather.15
  78.8 39.1 all-gather.17
  120.2 80.4 all-gather.19
  202.7 77.8 all-gather.21
  463.7 68.3 reduce-scatter.14
  535.5 68.7 reduce-scatter.16
  703.5 129.1 reduce-scatter.30
  894.0 129.3 reduce-scatter.32
  1027.0 160.8 reduce-scatter.20
  1191.3 161.2 reduce-scatter.18
  1356.1 161.2 reduce-scatter.24
  1520.8 161.2 reduce-scatter.22
  1685.3 62.3 reduce-scatter.26
  1751.5 61.1 reduce-scatter.28
  1816.0 78.8 all-reduce.38
  1900.9 120.8 all-reduce.36
where the time goes:
time: 2050 us; the launch traced here: 2030 us
  waiting for transfers between devices  1040 us (51%)
  matrix products  300 us (15%)
  local copies, waits for them, and re-layouts  217 us (11%)
  blocking collectives  209 us (10%)
  other arithmetic  176 us (9%)
  starting transfers between devices  62.9 us (3%)
  between operations  20.5 us (1%)
    reduce_scatter x2, waiting for transfers between devices, reduce_grads(): lax.psum_scatter(full_grads[9], 'fsdp', scatter_dimension=0, tiled=True)  325 us
    reduce_scatter x2, waiting for transfers between devices, reduce_grads(): lax.psum_scatter(full_grads[7], 'fsdp', scatter_dimension=0, tiled=True)  325 us
    psum x1, waiting for transfers between devices, body(): head_sums = lax.psum(head_total, ('seq', 'fsdp'))  121 us
    unnamed x429, local copies, waits for them, and re-layouts  96.9 us
    unnamed x18, waiting for transfers between devices  90.5 us
    reduce_scatter x2, waiting for transfers between devices, reduce_grads(): lax.psum_scatter(full_grads[13], 'fsdp', scatter_dimension=0, tiled=True)  80.3 us
    unnamed x2, blocking collectives  69.3 us
    convert_element_type x6, other arithmetic, backward_block(): grad_scores = (soft * (grad_soft - inner)).astype(jnp.bfloat16)  57.1 us
  transfers between devices with their start and end apart: 32, of which 19 were waited for; matrix products, arithmetic and copies ran while one was open for 29% of the time, Pallas kernels for 0%

commit v1 on v0

v1 whole, which is shorter than its diff:
```python
import jax
import jax.numpy as jnp
from jax import lax
from jax.sharding import PartitionSpec as P

HEAD_DIM = 64
highest = lax.Precision.HIGHEST
masked_value = -1e30
bf16 = jnp.bfloat16
f32 = jnp.float32


def factors(count):
    found = []
    while count % 4 == 0:
        found.append(4)
        count //= 4
    if count > 1:
        found.append(count)
    return sorted(found)


def ring_pairs(count, stride, radix):
    pairs = []
    for source in range(count):
        digit = (source // stride) % radix
        pairs.append((source, source + ((digit + 1) % radix - digit) * stride))
    return pairs


def swap(value, mask):
    count = lax.axis_size("seq")
    return lax.ppermute(value, "seq", [(i, i ^ mask) for i in range(count)])


def pair_stack(value, mask, bit, axis):
    other = swap(value, mask)
    return jnp.stack([jnp.where(bit == 0, value, other), jnp.where(bit == 0, other, value)], axis)


def ring_gather(value):
    count = lax.axis_size("fsdp")
    index = lax.axis_index("fsdp")
    total = value[None]
    stride = 1
    for radix in factors(count):
        digit = (index // stride) % radix
        pairs = ring_pairs(count, stride, radix)
        current = total
        parts = [total]
        for _ in range(radix - 1):
            current = lax.ppermute(current, "fsdp", pairs)
            parts.append(current)
        if radix == 2:
            stacked = jnp.stack(
                [jnp.where(digit == 0, parts[0], parts[1]), jnp.where(digit == 0, parts[1], parts[0])]
            )
        else:
            stacked = jnp.zeros((radix,) + total.shape, total.dtype)
            for step, part in enumerate(parts):
                stacked = lax.dynamic_update_index_in_dim(
                    stacked, part, lax.rem(digit - step + radix, radix), 0
                )
        total = stacked.reshape((radix * total.shape[0],) + value.shape)
        stride *= radix
    return total


def ring_scatter(value, wire=bf16):
    count = lax.axis_size("fsdp")
    index = lax.axis_index("fsdp")
    stride = 1
    for radix in factors(count):
        digit = (index // stride) % radix
        pairs = ring_pairs(count, stride, radix)
        view = value.reshape((value.shape[0] // radix, radix) + value.shape[1:])

        def own(offset):
            return lax.dynamic_index_in_dim(
                view, lax.rem(digit + offset + 2 * radix, radix), 1, keepdims=False
            )

        current = own(-1)
        for step in range(radix - 1):
            moved = lax.ppermute(current.astype(wire), "fsdp", pairs)
            current = own(-2 - step) + moved.astype(f32)
        value = current
        stride *= radix
    return value[0]


def ring_sum(value):
    count = lax.axis_size("fsdp")
    stride = 1
    for radix in factors(count):
        pairs = ring_pairs(count, stride, radix)
        index = (lax.axis_index("fsdp") // stride) % radix
        current = value
        parts = [value]
        for _ in range(radix - 1):
            current = lax.ppermute(current, "fsdp", pairs)
            parts.append(current)
        if radix == 2:
            value = parts[0] + parts[1]
        else:
            stacked = jnp.zeros((radix,) + value.shape, value.dtype)
            for step, part in enumerate(parts):
                stacked = lax.dynamic_update_index_in_dim(
                    stacked, part, lax.rem(index - step + radix, radix), 0
                )
            value = jnp.sum(stacked, axis=0)
        stride *= radix
    return value


def seq_sum(value, wire=f32):
    value = value + swap(value.astype(wire), 1).astype(f32)
    return value + swap(value.astype(wire), 2).astype(f32)


def by_seq(parts, chip, core):
    first = [
        jnp.where(core == 0, parts[0], parts[1]),
        jnp.where(core == 0, parts[1], parts[0]),
        jnp.where(core == 0, parts[2], parts[3]),
        jnp.where(core == 0, parts[3], parts[2]),
    ]
    return [
        jnp.where(chip == 0, first[0], first[2]),
        jnp.where(chip == 0, first[1], first[3]),
        jnp.where(chip == 0, first[2], first[0]),
        jnp.where(chip == 0, first[3], first[1]),
    ]


def gather_rows(shard, core):
    rows, columns = shard.shape
    half = rows // 2
    mine = lax.dynamic_slice_in_dim(shard, core * half, half)
    gathered = ring_gather(mine)
    return pair_stack(gathered, 1, core, 1).reshape(-1, columns)


def reduce_rows(grad, chip, core):
    rows, columns = grad.shape
    count = lax.axis_size("fsdp")
    half = rows // (2 * count)
    wide = columns // 2
    view = grad.reshape(count, 2, half, 2, wide)
    sent = lax.dynamic_index_in_dim(view, 1 - core, 1, keepdims=False).astype(bf16)
    kept = lax.dynamic_index_in_dim(view, core, 1, keepdims=False)
    kept = kept + swap(sent, 1).astype(f32)
    sent = lax.dynamic_index_in_dim(kept, 1 - chip, 2, keepdims=False).astype(bf16)
    kept = lax.dynamic_index_in_dim(kept, chip, 2, keepdims=False)
    kept = kept + swap(sent, 2).astype(f32)
    owned = ring_scatter(kept).astype(bf16)
    both = pair_stack(owned, 2, chip, 1)
    return pair_stack(both, 1, core, 0).reshape(2 * half, columns).astype(f32)


def layer_norm(values, gain, shift):
    center = values - jnp.mean(values, axis=-1, keepdims=True)
    spread = jnp.mean(center * center, axis=-1, keepdims=True)
    return center * lax.rsqrt(spread + 1e-06) * gain + shift


def exact_gelu(values):
    return jax.nn.gelu(values, approximate=False)


def segment_ids(order_row, length_row):
    ends = jnp.cumsum(length_row)
    above = (order_row[:, None] >= ends[None, :-1]).astype(jnp.int32)
    return jnp.sum(above, axis=1)


def classify(pooled, w_pool, bias_pool, w_class, bias_class, labels):
    inner = jnp.tanh(
        jnp.dot(pooled, w_pool, precision=highest, preferred_element_type=f32) + bias_pool
    )
    logits = jnp.dot(inner, w_class, precision=highest, preferred_element_type=f32) + bias_class
    row_peak = jnp.max(logits, axis=-1, keepdims=True)
    log_total = row_peak[:, 0] + jnp.log(jnp.sum(jnp.exp(logits - row_peak), axis=-1))
    classes = jnp.arange(logits.shape[1])
    picked = jnp.sum(jnp.where(classes[None, :] == labels[:, None], logits, 0.0), axis=-1)
    return (jnp.sum(log_total - picked), logits)


def big_product(left, right):
    return jnp.dot(left, right, preferred_element_type=f32)


def left_product(left, right):
    return lax.dot_general(left, right, (((0,), (0,)), ((), ())), preferred_element_type=f32)


def right_product(left, right):
    return lax.dot_general(left, right, (((1,), (1,)), ((), ())), preferred_element_type=f32)


def combine_parts(first, second):
    new_peak = jnp.maximum(first[0], second[0])
    first_scale = jnp.exp(first[0] - new_peak)
    second_scale = jnp.exp(second[0] - new_peak)
    return (
        new_peak,
        first[1] * first_scale + second[1] * second_scale,
        first[2] * first_scale[..., None] + second[2] * second_scale[..., None],
    )


def attention_forward(query, key, value, segments):
    tokens, width = query.shape
    heads = width // HEAD_DIM
    scaling = HEAD_DIM ** (-0.5)
    rows = min(512, tokens)
    blocks = tokens // rows
    key_all = key.reshape(tokens, heads, HEAD_DIM)
    value_all = value.reshape(tokens, heads, HEAD_DIM)

    def one_block(inputs):
        query_part, segment_part = inputs
        scores = jnp.einsum("qhd,khd->hqk", query_part, key_all, preferred_element_type=f32)
        same = (segment_part[:, None] == segments[None, :])[None]
        scores = jnp.where(same, scores * scaling, masked_value)
        peak = jnp.max(scores, axis=-1, keepdims=True)
        exponent = jnp.exp(scores - peak)
        totals = jnp.sum(exponent, axis=-1, keepdims=True)
        probs = (exponent / totals).astype(bf16)
        context = jnp.einsum("hqk,khd->qhd", probs, value_all, preferred_element_type=f32)
        return (context.astype(bf16), peak[:, :, 0] + jnp.log(totals[:, :, 0]))

    contexts, logs = lax.map(
        one_block,
        (query.reshape(blocks, rows, heads, HEAD_DIM), segments.reshape(blocks, rows)),
    )
    return contexts.reshape(tokens, width), logs


def attention_backward(query, key, value, segments, logs, grad_context):
    tokens, width = query.shape
    heads = width // HEAD_DIM
    scaling = HEAD_DIM ** (-0.5)
    rows = min(512, tokens)
    blocks = tokens // rows
    key_all = key.reshape(tokens, heads, HEAD_DIM)
    value_all = value.reshape(tokens, heads, HEAD_DIM)

    def one_block(carry, inputs):
        query_part, segment_part, log_part, grad_part = inputs
        scores = jnp.einsum("qhd,khd->hqk", query_part, key_all, preferred_element_type=f32)
        same = (segment_part[:, None] == segments[None, :])[None]
        soft = jnp.exp(jnp.where(same, scores * scaling, masked_value) - log_part[:, :, None])
        grad_soft = jnp.einsum("qhd,khd->hqk", grad_part, value_all, preferred_element_type=f32)
        inner = jnp.sum(soft * grad_soft, axis=-1, keepdims=True)
        grad_scores = (soft * (grad_soft - inner)).astype(bf16)
        grad_query = (
            jnp.einsum("hqk,khd->qhd", grad_scores, key_all, preferred_element_type=f32) * scaling
        )
        grad_key = carry[0] + scaling * jnp.einsum(
            "hqk,qhd->khd", grad_scores, query_part, preferred_element_type=f32
        )
        grad_value = carry[1] + jnp.einsum(
            "hqk,qhd->khd", soft.astype(bf16), grad_part, preferred_element_type=f32
        )
        return ((grad_key, grad_value), grad_query.astype(bf16))

    zeros = jnp.zeros((tokens, heads, HEAD_DIM), f32)
    (grad_key, grad_value), grad_query = lax.scan(
        one_block,
        (zeros, zeros),
        (
            query.reshape(blocks, rows, heads, HEAD_DIM),
            segments.reshape(blocks, rows),
            logs,
            grad_context.reshape(blocks, rows, heads, HEAD_DIM),
        ),
    )
    return jnp.concatenate(
        [
            grad_query.reshape(tokens, width),
            grad_key.astype(bf16).reshape(tokens, width),
            grad_value.astype(bf16).reshape(tokens, width),
        ],
        axis=1,
    )


def body(
    hidden_in,
    cotangent,
    lengths,
    slot_order,
    labels,
    w_qkv,
    bias_query,
    bias_value,
    w_out,
    bias_out,
    gain_attn,
    shift_attn,
    w_up,
    bias_up,
    w_down,
    bias_down,
    gain_ffn,
    shift_ffn,
    w_student,
    bias_student,
    pool_query,
    w_pool,
    bias_pool,
    w_class,
    bias_class,
):
    seq_count = lax.axis_size("seq")
    fsdp_count = lax.axis_size("fsdp")
    seq_index = lax.axis_index("seq")
    chip = seq_index // 2
    core = seq_index % 2
    micro = hidden_in.shape[0]
    tokens = hidden_in.shape[2]
    width = hidden_in.shape[3]
    group = slot_order.shape[2]
    docs = lengths.shape[2]
    pool_heads, pool_dim = pool_query.shape
    head_width = width // seq_count
    shard = w_qkv.shape[0]
    first_seq = (seq_index == 0).astype(f32)

    small_list = (
        bias_query,
        bias_value,
        bias_out,
        gain_attn,
        shift_attn,
        bias_up,
        bias_down,
        gain_ffn,
        shift_ffn,
        bias_student,
        w_student.reshape(-1),
    )
    small_all = ring_gather(jnp.concatenate(small_list))
    full_small = []
    start = 0
    for part in small_list:
        size = part.shape[0]
        full_small.append(small_all[:, start : start + size].reshape(-1))
        start += size
    (
        full_bias_query,
        full_bias_value,
        full_bias_out,
        full_gain_attn,
        full_shift_attn,
        full_bias_up,
        full_bias_down,
        full_gain_ffn,
        full_shift_ffn,
        full_bias_student,
    ) = [part.astype(f32) for part in full_small[:-1]]
    full_student = full_small[-1].reshape(width, -1)

    own_qkv_shard = lax.dynamic_index_in_dim(
        w_qkv.reshape(shard, 3, seq_count, head_width), seq_index, 2, keepdims=False
    ).reshape(shard, 3 * head_width)
    own_qkv = ring_gather(own_qkv_shard).reshape(width, 3 * head_width)
    own_bias = jnp.concatenate(
        [
            lax.dynamic_slice_in_dim(full_bias_query, seq_index * head_width, head_width),
            jnp.zeros((head_width,), f32),
            lax.dynamic_slice_in_dim(full_bias_value, seq_index * head_width, head_width),
        ]
    )

    hidden = hidden_in[:, 0]
    full_hidden = []
    for m in range(micro):
        both = pair_stack(hidden[m], 2, chip, 0)
        full_hidden.append(pair_stack(both, 1, core, 1).reshape(group, width))

    full_out = gather_rows(w_out, core)
    full_up = gather_rows(w_up, core)
    full_down = gather_rows(w_down, core)

    segments = [segment_ids(slot_order[m, 0], lengths[m, 0]) for m in range(micro)]

    saved = []
    context_parts = []
    for m in range(micro):
        projected = (big_product(full_hidden[m], own_qkv) + own_bias).astype(bf16)
        query = projected[:, :head_width]
        key = projected[:, head_width : 2 * head_width]
        value = projected[:, 2 * head_width :]
        context_own, logs = attention_forward(query, key, value, segments[m])
        saved.append((query, key, value, logs))
        view = context_own.reshape(seq_count, tokens, head_width)
        parts = []
        for mask in range(seq_count):
            part = lax.dynamic_index_in_dim(view, seq_index ^ mask, 0, keepdims=False)
            parts.append(part if mask == 0 else swap(part, mask))
        context_parts.append(jnp.concatenate(parts, axis=1))
    context = jnp.concatenate(context_parts, axis=0)
    out_view = full_out.reshape(seq_count, head_width, width)
    out_turned = jnp.concatenate(
        [
            lax.dynamic_index_in_dim(out_view, seq_index ^ mask, 0, keepdims=False)
            for mask in range(seq_count)
        ],
        axis=0,
    )
    branch = big_product(context, out_turned) + full_bias_out
    hidden_rows = hidden.reshape(micro * tokens, width)
    normed, first_norm_back = jax.vjp(
        layer_norm, hidden_rows.astype(f32) + branch, full_gain_attn, full_shift_attn
    )
    normed_low = normed.astype(bf16)
    upward = big_product(normed_low, full_up) + full_bias_up
    active, gelu_back = jax.vjp(exact_gelu, upward)
    active_low = active.astype(bf16)
    downward = big_product(active_low, full_down) + full_bias_down
    final, second_norm_back = jax.vjp(
        layer_norm, normed + downward, full_gain_ffn, full_shift_ffn
    )
    final_low = final.astype(bf16)

    student = big_product(final_low, full_student) + full_bias_student
    pieces = student.reshape(micro, tokens, pool_heads, pool_dim)
    energy = jnp.sum(pieces * pool_query, axis=-1)
    segment_local = jnp.stack(
        [lax.dynamic_slice_in_dim(part, seq_index * tokens, tokens) for part in segments]
    )
    members = (segment_local[:, :, None] == jnp.arange(docs, dtype=jnp.int32))[..., None]
    local_peak = jnp.max(jnp.where(members, energy[:, :, None, :], masked_value), axis=1)
    local_weights = jnp.exp(
        jnp.where(members, energy[:, :, None, :] - local_peak[:, None], masked_value)
    )
    local_total = jnp.sum(local_weights, axis=1)
    local_accum = jnp.einsum("btnh,bthd->bnhd", local_weights, pieces, precision=highest)
    packed = jnp.concatenate([local_peak[..., None], local_total[..., None], local_accum], axis=-1)
    for mask in (1, 2):
        other = swap(packed, mask)
        peak, total, accum = combine_parts(
            (packed[..., 0], packed[..., 1], packed[..., 2:]),
            (other[..., 0], other[..., 1], other[..., 2:]),
        )
        packed = jnp.concatenate([peak[..., None], total[..., None], accum], axis=-1)
    global_peak, global_total, global_accum = packed[..., 0], packed[..., 1], packed[..., 2:]
    pooled_heads = global_accum / global_total[..., None]
    pooled = pooled_heads.reshape(micro * docs, -1)

    def head_loss(pooled_rows, pool_weight, pool_bias, class_weight, class_bias):
        return classify(
            pooled_rows, pool_weight, pool_bias, class_weight, class_bias, labels.reshape(-1)
        )

    loss_value, head_back, logit_rows = jax.vjp(
        head_loss, pooled, w_pool, bias_pool, w_class, bias_class, has_aux=True
    )
    logits = logit_rows.reshape(micro, 1, docs, -1)
    grad_pooled, grad_wpool, grad_bpool, grad_wclass, grad_bclass = head_back(
        jnp.ones_like(loss_value)
    )
    alpha = (
        jnp.exp(jnp.where(members, energy[:, :, None, :] - global_peak[:, None], masked_value))
        / global_total[:, None]
    )
    grad_heads = grad_pooled.reshape(micro, docs, pool_heads, pool_dim)
    along = jnp.einsum("bthd,bnhd->btnh", pieces, grad_heads, precision=highest)
    baseline = jnp.sum(pooled_heads * grad_heads, axis=-1)
    grad_energy = jnp.sum(alpha * (along - baseline[:, None]), axis=2)
    grad_pieces = (
        jnp.einsum("btnh,bnhd->bthd", alpha, grad_heads, precision=highest)
        + grad_energy[..., None] * pool_query
    )
    grad_pool_query = jnp.einsum("bth,bthd->hd", grad_energy, pieces, precision=highest)
    grad_student = grad_pieces.reshape(micro * tokens, -1).astype(bf16)
    grad_w_student = left_product(final_low, grad_student)
    grad_bias_student = jnp.sum(grad_student.astype(f32), axis=0)

    cotangent_rows = cotangent[:, 0].reshape(micro * tokens, width)
    grad_final = cotangent_rows.astype(f32) + right_product(grad_student, full_student)
    grad_mid, grad_gain_ffn, grad_shift_ffn = second_norm_back(grad_final)
    grad_down = grad_mid.astype(bf16)
    grad_bias_down = jnp.sum(grad_down.astype(f32), axis=0)
    grad_w_down = left_product(active_low, grad_down)
    (grad_upward,) = gelu_back(right_product(grad_down, full_down))
    grad_up = grad_upward.astype(bf16)
    grad_bias_up = jnp.sum(grad_up.astype(f32), axis=0)
    grad_w_up = left_product(normed_low, grad_up)
    grad_normed = grad_mid + right_product(grad_up, full_up)
    grad_res, grad_gain_attn, grad_shift_attn = first_norm_back(grad_normed)
    grad_branch = grad_res.astype(bf16)
    grad_bias_out = jnp.sum(grad_branch.astype(f32), axis=0)
    grad_out_turned = left_product(context, grad_branch).reshape(seq_count, head_width, width)
    grad_w_out = jnp.concatenate(
        by_seq([grad_out_turned[m] for m in range(seq_count)], chip, core), axis=0
    )
    grad_context = right_product(grad_branch, out_turned).astype(bf16)

    grad_own_qkv = None
    grad_bias_own = None
    grad_inputs = []
    for m in range(micro):
        rows = grad_context[m * tokens : (m + 1) * tokens]
        parts = []
        for mask in range(seq_count):
            part = rows[:, mask * head_width : (mask + 1) * head_width]
            parts.append(part if mask == 0 else swap(part, mask))
        grad_context_own = jnp.concatenate(by_seq(parts, chip, core), axis=0)
        query, key, value, logs = saved[m]
        grad_proj = attention_backward(query, key, value, segments[m], logs, grad_context_own)
        bias_sum = jnp.sum(grad_proj.astype(f32), axis=0)
        weight_sum = left_product(full_hidden[m], grad_proj)
        grad_bias_own = bias_sum if grad_bias_own is None else grad_bias_own + bias_sum
        grad_own_qkv = weight_sum if grad_own_qkv is None else grad_own_qkv + weight_sum
        partial = right_product(grad_proj, own_qkv).reshape(2, 2, tokens, width)
        sent = lax.dynamic_index_in_dim(partial, 1 - core, 1, keepdims=False).astype(bf16)
        kept = lax.dynamic_index_in_dim(partial, core, 1, keepdims=False)
        kept = kept + swap(sent, 1).astype(f32)
        sent = lax.dynamic_index_in_dim(kept, 1 - chip, 0, keepdims=False).astype(bf16)
        kept = lax.dynamic_index_in_dim(kept, chip, 0, keepdims=False)
        kept = kept + swap(sent, 2).astype(f32)
        grad_inputs.append(grad_res[m * tokens : (m + 1) * tokens] + kept)

    out_w_down = reduce_rows(grad_w_down, chip, core)
    out_w_up = reduce_rows(grad_w_up, chip, core)
    out_w_out = reduce_rows(grad_w_out, chip, core)
    owned_qkv = ring_scatter(grad_own_qkv.reshape(fsdp_count, shard, 3 * head_width)).astype(bf16)
    both = pair_stack(owned_qkv.reshape(shard, 3, head_width), 2, chip, 2)
    out_w_qkv = pair_stack(both, 1, core, 3).reshape(shard, 3 * width).astype(f32)

    early = (
        grad_bias_out,
        grad_gain_attn,
        grad_shift_attn,
        grad_bias_up,
        grad_bias_down,
        grad_gain_ffn,
        grad_shift_ffn,
        grad_bias_student,
        grad_w_student.reshape(-1),
    )
    early_packed = jnp.concatenate([part.reshape(fsdp_count, -1) for part in early], axis=1)
    early_owned = ring_scatter(seq_sum(early_packed, bf16))
    placed_bias = jnp.zeros((2, seq_count, head_width), f32)
    placed_bias = lax.dynamic_update_slice(
        placed_bias,
        grad_bias_own.reshape(3, 1, head_width)[::2],
        (0, seq_index, 0),
    ).reshape(2, fsdp_count, -1)
    late_packed = jnp.concatenate([placed_bias[0], placed_bias[1]], axis=1)
    late_owned = ring_scatter(seq_sum(late_packed), f32)
    early_out = []
    start = 0
    for part in early:
        size = part.size // fsdp_count
        early_out.append(early_owned[start : start + size])
        start += size
    bias_size = late_owned.shape[0] // 2

    query_total = seq_sum(grad_pool_query)
    head_list = (query_total, grad_wpool, grad_bpool, grad_wclass, grad_bclass)
    head_packed = ring_sum(jnp.concatenate([part.reshape(-1) for part in head_list]))
    head_out = []
    start = 0
    for part in head_list:
        head_out.append(head_packed[start : start + part.size].reshape(part.shape))
        start += part.size

    return (
        final_low.reshape(micro, 1, tokens, width),
        logits,
        jnp.stack(grad_inputs)[:, None],
        out_w_qkv,
        late_owned[:bias_size],
        late_owned[bias_size:],
        out_w_out,
        early_out[0],
        early_out[1],
        early_out[2],
        out_w_up,
        early_out[3],
        out_w_down,
        early_out[4],
        early_out[5],
        early_out[6],
        early_out[8].reshape(w_student.shape),
        early_out[7],
    ) + tuple(head_out)


def solution(mesh):
    rows, vector = P("fsdp", None), P("fsdp")
    sharded = (
        rows, vector, vector, rows, vector, vector, vector, rows,
        vector, rows, vector, vector, vector, rows, vector,
    )
    return jax.shard_map(
        body,
        mesh=mesh,
        in_specs=(P(None, "fsdp", "seq", None),) * 2
        + (P(None, "fsdp", None),) * 3
        + sharded
        + (P(),) * 5,
        out_specs=(
            P(None, "fsdp", "seq", None),
            P(None, "fsdp", None, None),
            P(None, "fsdp", "seq", None),
        )
        + sharded
        + (P(),) * 5,
        check_vma=False,
    )
```

time: 2050 us -> 949 us (0.46)
  waiting for transfers between devices: 1040 us -> 250 us
  blocking collectives: 209 us -> 0 us
  matrix products: 300 us -> 259 us
  other arithmetic: 176 us -> 140 us
    reduce_scatter x8 -> x0, waiting for transfers between devices: 730 us -> none  [the longest x2 325 us: reduce_grads(): lax.psum_scatter(full_grads[9], 'fsdp', scatter_dimension=0, tiled=True)]
    ppermute x0 -> x93, waiting for transfers between devices: none -> 250 us  [the longest x24 98.1 us: ring_scatter(): moved = lax.ppermute(current.astype(wire), 'fsdp', pairs)]
    psum x2 -> x0, waiting for transfers between devices: 139 us -> none  [the longest x1 121 us: body(): head_sums = lax.psum(head_total, ('seq', 'fsdp'))]
    unnamed x18 -> x0, waiting for transfers between devices: 90.5 us -> none
    all_gather x8 -> x0, blocking collectives: 88.3 us -> none  [the longest x1 32.1 us: fetch_forward(): lax.all_gather(shards[13], 'fsdp', axis=0, tiled=True)]
    unnamed x2 -> x0, blocking collectives: 69.3 us -> none
    ppermute x0 -> x93, starting transfers between devices: none -> 69 us  [the longest x45 24.5 us: swap(): return lax.ppermute(value, 'seq', [(i, i ^ mask) for i in range(count)])]
    unnamed x429 -> x278, local copies, waits for them, and re-layouts: 96.9 us -> 29.2 us
  transfers between devices with their start and end apart: 32 -> 93, of which waited for: 19 -> 45; matrix products, arithmetic and copies ran while one was open for 29% -> 48% of each run, Pallas kernels for 0% -> 0%
where the time goes in v1:
time: 949 us; the launch traced here: 932 us
  matrix products  259 us (27%)
  waiting for transfers between devices  250 us (26%)
  local copies, waits for them, and re-layouts  209 us (22%)
  other arithmetic  140 us (15%)
  starting transfers between devices  69 us (7%)
    ppermute x24, waiting for transfers between devices, ring_scatter(): moved = lax.ppermute(current.astype(wire), 'fsdp', pairs)  98.1 us
    ppermute x45, waiting for transfers between devices, swap(): return lax.ppermute(value, 'seq', [(i, i ^ mask) for i in range(count)])  85.3 us
    ppermute x20, waiting for transfers between devices, ring_gather(): current = lax.ppermute(current, 'fsdp', pairs)  64.9 us
    convert_element_type x6, other arithmetic, one_block(): grad_scores = (soft * (grad_soft - inner)).astype(bf16)  56.7 us
    dot_general x12, matrix products, one_block(): jnp.einsum('qhd,khd->hqk', query_part, key_all, preferred_element_type=f32)  55.9 us
    dot_general x6, matrix products, big_product(): return jnp.dot(left, right, preferred_element_type=f32)  40.9 us
    dot_general x6, matrix products, right_product(): lax.dot_general(left, right, (((1,), (1,)), ((), ())), preferred_element_...  30.9 us
    reshape x3, local copies, waits for them, and re-layouts, reduce_rows(): view = grad.reshape(count, 2, half, 2, wide)  29.7 us
  transfers between devices with their start and end apart: 93, of which 45 were waited for; matrix products, arithmetic and copies ran while one was open for 48% of the time, Pallas kernels for 0%

profile of v1, /device:TPU:8, one launch (start us, length us, event | category | flops | bytes accessed | tf_op | source)
XLA Modules:
  0.0 932.4 jit_solution(3380040563746916901)
XLA Ops:
  0.7 7.6 concatenate.66
  66.3 20.3 %collective-permute-done.21 = bf16[2,48,768]{2,1,0:T(8,128)(2,1)S(1)} collective-permute-done((bf16[2,48,768]{2,1,0:T(8,128)(2,1)}, bf16[2,48,768]{2,1,0:T(8,128)(2,1)S(1)}, u32[]{:S(2)}, u32[]{:S(2)}) %collective-permute-start.21) | collective-permute-done | bytes 147488 | tf_op jit(solution)/shard_map/ppermute | solution.py:52
  117.9 10.2 %collective-permute-done.25 = bf16[2,48,3072]{2,1,0:T(8,128)(2,1)} collective-permute-done((bf16[2,48,3072]{2,1,0:T(8,128)(2,1)}, bf16[2,48,3072]{2,1,0:T(8,128)(2,1)}, u32[]{:S(2)}, u32[]{:S(2)}) %collective-permute-start.25) | collective-permute-done | bytes 589856 | tf_op jit(solution)/shard_map/ppermute | solution.py:52
  128.1 12.6 %collective-permute-done.30 = bf16[2,192,768]{2,1,0:T(8,128)(2,1)} collective-permute-done((bf16[2,192,768]{2,1,0:T(8,128)(2,1)}, bf16[2,192,768]{2,1,0:T(8,128)(2,1)}, u32[]{:S(2)}, u32[]{:S(2)}) %collective-permute-start.30) | collective-permute-done | bytes 589856 | tf_op jit(solution)/shard_map/ppermute | solution.py:52
  153.0 26.9 %while.55 = (s32[]{:T(128)}, bf16[3,512,3,64]{1,3,2,0:T(8,128)(2,1)S(1)}, f32[3,3,512]{2,1,0:T(4,128)S(1)}, s32[3,512]{1,0:T(4,128)S(1)}, s32[1536]{0:T(1024)S(1...) while((s32[]{:T(128)}, ...), condition=%wide.region_11.12_spmd, body=%wide.region_8.11_spmd.sunk | while | flops 633174528 | bytes 33101940 | solution.py:233
  199.4 27.3 %while.54 = (s32[]{:T(128)}, bf16[3,512,3,64]{1,3,2,0:T(8,128)(2,1)S(1)}, f32[3,3,512]{2,1,0:T(4,128)S(1)}, s32[3,512]{1,0:T(4,128)S(1)}, s32[1536]{0:T(1024)S(1...) while((s32[]{:T(128)}, ...), condition=%wide.region_5.6_spmd, body=%wide.region_2.5_spmd.sunk | while | flops 633174528 | bytes 33101940 | solution.py:233
  251.5 26.8 %multiply_convert_fusion.2 = (bf16[768,3072]{1,0:T(8,128)(2,1)S(1)}, f32[768,3072]{1,0:T(8,128)}, f32[768,3072]{1,0:T(8,128)}) fusion(f32[3072]{0:T(1024)S(1)} %copy-done.105, bf16[768,3072]{1,0:T(8,128)(2,1)S(1)} %bitcast.694, f32[768,768]{1,0:T(8,128)S(1)} %get-tuple-element.786, f32[768]{0:T(1024)S(1)} %copy-done.84, f32[768]{0:T(1024)S(1)} %copy-done.82, ...), kind=kOutput, calls=%fused_computation.100 | convolution fusion | flops 3782541312 | bytes 30695424 | tf_op jit(solution)/shard_map/dot_general | solution.py:190
  302.8 13.3 %convert_reduce_fusion = (f32[3072]{0:T(1024)S(1)}, bf16[768,3072]{1,0:T(8,128)(2,1)}) fusion(f32[768,3072]{1,0:T(8,128)} %get-tuple-element.668, f32[768,3072]{1,0:T(8,128)} %get-tuple-element.787, f32[3072]{0:T(1024)S(1)} %copy-done.105, bf16[768,768]{1,0:T(8,128)(2,1)} %get-tuple-element.654, bf16[3072,768]{1,0:T(8,128)(2,1)S(1)} %bitcast.701), kind=kOutput, calls=%fused_computation.98 | convolution fusion | flops 3663983616 | bytes 29515776 | tf_op jit(solution)/shard_map/dot_general | solution.py:198
  316.1 8.4 multiply_reduce_fusion.3
  331.5 8.8 fusion.191
  340.3 13.4 %reshape.857 = f32[8,2,48,2,1536]{4,3,2,1,0:T(2,128)} reshape(f32[768,3072]{1,0:T(8,128)} %fusion.172) | data formatting | bytes 18874368 | tf_op jit(solution)/shard_map/reshape | solution.py:149
  365.0 12.5 %reshape.859 = f32[8,2,192,2,384]{4,3,2,1,0:T(2,128)} reshape(f32[3072,768]{1,0:T(8,128)} %fusion.191) | data formatting | bytes 18874368 | tf_op jit(solution)/shard_map/reshape | solution.py:149
  435.5 96.6 %while.56 = (s32[]{:T(128)}, f32[1536,3,64]{0,2,1:T(8,128)S(1)}, f32[1536,3,64]{0,2,1:T(8,128)S(1)}, bf16[3,512,3,64]{1,3,2,0:T(8,128)(2,1)}, bf16[3,512,3,64]{1...) while((s32[]{:T(128)}, f32[1536,3,64]{0,2,1:T(8,128)S(1)}, ...), condition=%wide.region_31.32_spmd.clone, body=%wide.region_29.31_spmd.clone.sunk | while | flops 1533639168 | bytes 131770624 | solution.py:269
  447.4 9.5 %multiply_convert_fusion.5 = bf16[3,512,1536]{2,1,0:T(8,128)(2,1)} fusion(f32[3,512,1536]{2,1,0:T(8,128)} %get-tuple-element.1033, f32[3,512,1536]{2,1,0:T(8,128)} %copy-done.2, f32[3,512]{1,0:T(4,128)S(1)} %get-tuple-element.1034), kind=kLoop, calls=%fused_computation.36.clone.1 | loop fusion | flops 7077888 | bytes 23599104 | tf_op jit(solution)/shard_map/while/body/eval_jaxpr/convert_element_type | solution.py:256
  479.6 9.5 %multiply_convert_fusion.5 = bf16[3,512,1536]{2,1,0:T(8,128)(2,1)} fusion(f32[3,512,1536]{2,1,0:T(8,128)} %get-tuple-element.1033, f32[3,512,1536]{2,1,0:T(8,128)} %copy-done.2, f32[3,512]{1,0:T(4,128)S(1)} %get-tuple-element.1034), kind=kLoop, calls=%fused_computation.36.clone.1 | loop fusion | flops 7077888 | bytes 23599104 | tf_op jit(solution)/shard_map/while/body/eval_jaxpr/convert_element_type | solution.py:256
  511.8 9.5 %multiply_convert_fusion.5 = bf16[3,512,1536]{2,1,0:T(8,128)(2,1)} fusion(f32[3,512,1536]{2,1,0:T(8,128)} %get-tuple-element.1033, f32[3,512,1536]{2,1,0:T(8,128)} %copy-done.2, f32[3,512]{1,0:T(4,128)S(1)} %get-tuple-element.1034), kind=kLoop, calls=%fused_computation.36.clone.1 | loop fusion | flops 7077888 | bytes 23599104 | tf_op jit(solution)/shard_map/while/body/eval_jaxpr/convert_element_type | solution.py:256
  568.6 96.2 %while.57 = (s32[]{:T(128)}, f32[1536,3,64]{0,2,1:T(8,128)S(1)}, f32[1536,3,64]{0,2,1:T(8,128)S(1)}, bf16[3,512,3,64]{1,3,2,0:T(8,128)(2,1)}, bf16[3,512,3,64]{1...) while((s32[]{:T(128)}, f32[1536,3,64]{0,2,1:T(8,128)S(1)}, ...), condition=%wide.region_34.35_spmd.clone, body=%wide.region_32.34_spmd.clone.sunk | while | flops 1533639168 | bytes 131770624 | solution.py:269
  573.3 7.3 multiply_reduce_fusion.13
  580.6 9.4 %multiply_convert_fusion.6 = bf16[3,512,1536]{2,1,0:T(8,128)(2,1)} fusion(f32[3,512,1536]{2,1,0:T(8,128)} %get-tuple-element.1046, f32[3,512,1536]{2,1,0:T(8,128)} %copy-done.3, f32[3,512]{1,0:T(4,128)S(1)} %get-tuple-element.1047), kind=kLoop, calls=%fused_computation.66.clone.1 | loop fusion | flops 7077888 | bytes 23599104 | tf_op jit(solution)/shard_map/while/body/eval_jaxpr/convert_element_type | solution.py:256
  612.6 9.4 %multiply_convert_fusion.6 = bf16[3,512,1536]{2,1,0:T(8,128)(2,1)} fusion(f32[3,512,1536]{2,1,0:T(8,128)} %get-tuple-element.1046, f32[3,512,1536]{2,1,0:T(8,128)} %copy-done.3, f32[3,512]{1,0:T(4,128)S(1)} %get-tuple-element.1047), kind=kLoop, calls=%fused_computation.66.clone.1 | loop fusion | flops 7077888 | bytes 23599104 | tf_op jit(solution)/shard_map/while/body/eval_jaxpr/convert_element_type | solution.py:256
  644.7 9.4 %multiply_convert_fusion.6 = bf16[3,512,1536]{2,1,0:T(8,128)(2,1)} fusion(f32[3,512,1536]{2,1,0:T(8,128)} %get-tuple-element.1046, f32[3,512,1536]{2,1,0:T(8,128)} %copy-done.3, f32[3,512]{1,0:T(4,128)S(1)} %get-tuple-element.1047), kind=kLoop, calls=%fused_computation.66.clone.1 | loop fusion | flops 7077888 | bytes 23599104 | tf_op jit(solution)/shard_map/while/body/eval_jaxpr/convert_element_type | solution.py:256
  826.5 33.7 %collective-permute-done.44 = bf16[384,768]{1,0:T(8,128)(2,1)S(1)} collective-permute-done((bf16[384,768]{1,0:T(8,128)(2,1)S(1)}, bf16[384,768]{1,0:T(8,128)(2,1)S(1)}, u32[]{:S(2)}, u32[]{:S(2)}) %collective-permute-start.44) | collective-permute-done | bytes 589856 | tf_op jit(solution)/shard_map/ppermute | solution.py:33
  863.4 21.5 %collective-permute-done.80 = bf16[8,192,384]{2,1,0:T(8,128)(2,1)S(1)} collective-permute-done((bf16[8,192,384]{2,1,0:T(8,128)(2,1)S(1)}, bf16[8,192,384]{2,1,0:T(8,128)(2,1)S(1)}, u32[]{:S(2)}, u32[]{:S(2)}) %collective-permute-start.80) | collective-permute-done | bytes 1179680 | tf_op jit(solution)/shard_map/ppermute | solution.py:33
  886.0 14.0 %collective-permute-done.81 = bf16[4,192,384]{2,1,0:T(8,128)(2,1)S(1)} collective-permute-done((bf16[4,192,384]{2,1,0:T(8,128)(2,1)S(1)}, bf16[4,192,384]{2,1,0:T(8,128)(2,1)S(1)}, u32[]{:S(2)}, u32[]{:S(2)}) %collective-permute-start.81) | collective-permute-done | bytes 589856 | tf_op jit(solution)/shard_map/ppermute | solution.py:85
  (938 shorter events, 660.2 us)
Async XLA Ops:
  11.0 38.3 %collective-permute-start.23 = (bf16[1,48,3072]{2,1,0:T(8,128)(2,1)S(1)}, bf16[1,48,3072]{2,1,0:T(8,128)(2,1)S(1)}, u32[]{:S(2)}, u32[]{:S(2)}) collective-permute-start(bf16[1,48,3072]{2,1,0:T(8,128)(2,1)S(1)} %dynamic-slice_bitcast_fusion.3), channel_id=1, source_target_pairs={{0,1},{1,0},{2,3},{3,2},{4,5},{5,4},{6,7},{7,6},{8,9},{9,8},{10,11... | collective-permute-start | bytes 884744 | tf_op jit(solution)/shard_map/ppermute | solution.py:52
  16.3 79.7 %collective-permute-start = (bf16[384,768]{1,0:T(8,128)(2,1)}, bf16[384,768]{1,0:T(8,128)(2,1)}, u32[]{:S(2)}, u32[]{:S(2)}) collective-permute-start(bf16[384,768]{1,0:T(8,128)(2,1)} %get-tuple-element.717), channel_id=1, source_target_pairs={{0,16},{8,24},{16,0},{24,8},{1,17},{9,25},{17,1},{25,9},{2,18},{10... | collective-permute-start | bytes 1769480 | tf_op jit(solution)/shard_map/ppermute | solution.py:33
  17.8 78.2 %collective-permute-start.13 = (bf16[384,768]{1,0:T(8,128)(2,1)}, bf16[384,768]{1,0:T(8,128)(2,1)}, u32[]{:S(2)}, u32[]{:S(2)}) collective-permute-start(bf16[384,768]{1,0:T(8,128)(2,1)} %get-tuple-element.718), channel_id=1, source_target_pairs={{0,16},{8,24},{16,0},{24,8},{1,17},{9,25},{17,1},{25,9},{2,18},{10... | collective-permute-start | bytes 1769480 | tf_op jit(solution)/shard_map/ppermute | solution.py:33
  54.9 55.2 %collective-permute-start.24 = (bf16[2,48,3072]{2,1,0:T(8,128)(2,1)}, bf16[2,48,3072]{2,1,0:T(8,128)(2,1)}, u32[]{:S(2)}, u32[]{:S(2)}) collective-permute-start(bf16[2,48,3072]{2,1,0:T(8,128)(2,1)} %fusion.119), channel_id=1, source_target_pairs={{0,2},{1,3},{2,4},{3,5},{4,6},{5,7},{6,0},{7,1},{8,10},{9,11},{10,... | collective-permute-start | bytes 1769480 | tf_op jit(solution)/shard_map/ppermute | solution.py:52
  61.1 50.1 %collective-permute-start.29 = (bf16[2,192,768]{2,1,0:T(8,128)(2,1)}, bf16[2,192,768]{2,1,0:T(8,128)(2,1)}, u32[]{:S(2)}, u32[]{:S(2)}) collective-permute-start(bf16[2,192,768]{2,1,0:T(8,128)(2,1)} %fusion.118), channel_id=1, source_target_pairs={{0,2},{1,3},{2,4},{3,5},{4,6},{5,7},{6,0},{7,1},{8,10},{9,11},{10,... | collective-permute-start | bytes 1769480 | tf_op jit(solution)/shard_map/ppermute | solution.py:52
  99.0 44.8 %collective-permute-start.14 = (bf16[2,384,768]{2,1,0:T(8,128)(2,1)}, bf16[2,384,768]{2,1,0:T(8,128)(2,1)}, u32[]{:S(2)}, u32[]{:S(2)}) collective-permute-start(bf16[2,384,768]{2,1,0:T(8,128)(2,1)} %pad_maximum_fusion.8), channel_id=1, source_target_pairs={{0,8},{8,0},{16,24},{24,16},{1,9},{9,1},{17,25},{25,17},{2,10},{10... | collective-permute-start | bytes 3538952 | tf_op jit(solution)/shard_map/ppermute | solution.py:33
  107.5 83.5 %collective-permute-start.1 = (bf16[2,384,768]{2,1,0:T(8,128)(2,1)}, bf16[2,384,768]{2,1,0:T(8,128)(2,1)}, u32[]{:S(2)}, u32[]{:S(2)}) collective-permute-start(bf16[2,384,768]{2,1,0:T(8,128)(2,1)} %pad_maximum_fusion.7), channel_id=1, source_target_pairs={{0,8},{8,0},{16,24},{24,16},{1,9},{9,1},{17,25},{25,17},{2,10},{10... | collective-permute-start | bytes 3538952 | tf_op jit(solution)/shard_map/ppermute | solution.py:33
  128.1 69.1 %collective-permute-start.26 = (bf16[2,48,3072]{2,1,0:T(8,128)(2,1)}, bf16[2,48,3072]{2,1,0:T(8,128)(2,1)}, u32[]{:S(2)}, u32[]{:S(2)}) collective-permute-start(bf16[2,48,3072]{2,1,0:T(8,128)(2,1)} %collective-permute-done.25), channel_id=1, source_target_pairs={{0,2},{1,3},{2,4},{3,5},{4,6},{5,7},{6,0},{7,1},{8,10},{9,11},{10,... | collective-permute-start | bytes 1769480 | tf_op jit(solution)/shard_map/ppermute | solution.py:52
  140.8 91.3 %collective-permute-start.31 = (bf16[2,192,768]{2,1,0:T(8,128)(2,1)}, bf16[2,192,768]{2,1,0:T(8,128)(2,1)}, u32[]{:S(2)}, u32[]{:S(2)}) collective-permute-start(bf16[2,192,768]{2,1,0:T(8,128)(2,1)} %collective-permute-done.30), channel_id=1, source_target_pairs={{0,2},{1,3},{2,4},{3,5},{4,6},{5,7},{6,0},{7,1},{8,10},{9,11},{10,... | collective-permute-start | bytes 1769480 | tf_op jit(solution)/shard_map/ppermute | solution.py:52
  188.1 41.9 %collective-permute-start.17 = (bf16[384,192]{0,1:T(8,128)(2,1)}, bf16[384,192]{0,1:T(8,128)(2,1)}, u32[]{:S(2)}, u32[]{:S(2)}) collective-permute-start(bf16[384,192]{0,1:T(8,128)(2,1)} %bitcast.575), channel_id=1, source_target_pairs={{0,24},{8,16},{16,8},{24,0},{1,25},{9,17},{17,9},{25,1},{2,26},{10... | collective-permute-start | bytes 442376 | tf_op jit(solution)/shard_map/ppermute | solution.py:33
  188.8 42.7 %collective-permute-start.16 = (bf16[384,192]{0,1:T(8,128)(2,1)}, bf16[384,192]{0,1:T(8,128)(2,1)}, u32[]{:S(2)}, u32[]{:S(2)}) collective-permute-start(bf16[384,192]{0,1:T(8,128)(2,1)} %bitcast.576), channel_id=1, source_target_pairs={{0,16},{8,24},{16,0},{24,8},{1,17},{9,25},{17,1},{25,9},{2,18},{10... | collective-permute-start | bytes 442376 | tf_op jit(solution)/shard_map/ppermute | solution.py:33
  190.9 43.1 %collective-permute-start.15 = (bf16[384,192]{0,1:T(8,128)(2,1)}, bf16[384,192]{0,1:T(8,128)(2,1)}, u32[]{:S(2)}, u32[]{:S(2)}) collective-permute-start(bf16[384,192]{0,1:T(8,128)(2,1)} %bitcast.577), channel_id=1, source_target_pairs={{0,8},{8,0},{16,24},{24,16},{1,9},{9,1},{17,25},{25,17},{2,10},{10... | collective-permute-start | bytes 442376 | tf_op jit(solution)/shard_map/ppermute | solution.py:33
  199.2 43.2 %collective-permute-start.27 = (bf16[8,48,3072]{2,1,0:T(8,128)(2,1)}, bf16[8,48,3072]{2,1,0:T(8,128)(2,1)}, u32[]{:S(2)}, u32[]{:S(2)}) collective-permute-start(bf16[8,48,3072]{2,1,0:T(8,128)(2,1)} %bitcast.676), channel_id=1, source_target_pairs={{0,8},{8,0},{16,24},{24,16},{1,9},{9,1},{17,25},{25,17},{2,10},{10... | collective-permute-start | bytes 7077896 | tf_op jit(solution)/shard_map/ppermute | solution.py:33
  406.7 327.2 %collective-permute-start.57 = (bf16[8,48,2,384]{3,1,0,2:T(8,128)(2,1)}, bf16[8,48,2,384]{3,1,0,2:T(8,128)(2,1)}, u32[]{:S(2)}, u32[]{:S(2)}) collective-permute-start(bf16[8,48,2,384]{3,1,0,2:T(8,128)(2,1)} %bitcast.574), channel_id=1, source_target_pairs={{0,8},{8,0},{16,24},{24,16},{1,9},{9,1},{17,25},{25,17},{2,10},{10... | collective-permute-start | bytes 1769480 | tf_op jit(solution)/shard_map/ppermute | solution.py:33
  421.8 127.2 %collective-permute-start.65 = (bf16[8,13264]{1,0:T(8,128)(2,1)}, bf16[8,13264]{1,0:T(8,128)(2,1)}, u32[]{:S(2)}, u32[]{:S(2)}) collective-permute-start(bf16[8,13264]{1,0:T(8,128)(2,1)} %convert_element_type.609), channel_id=1, source_target_pairs={{0,8},{8,0},{16,24},{24,16},{1,9},{9,1},{17,25},{25,17},{2,10},{10... | collective-permute-start | bytes 636680 | tf_op jit(solution)/shard_map/ppermute | solution.py:33
  424.6 120.2 %collective-permute-start.90 = (f32[18446]{0:T(1024)S(1)}, f32[18446]{0:T(1024)}, u32[]{:S(2)}, u32[]{:S(2)}) collective-permute-start(f32[18446]{0:T(1024)S(1)} %add.792), channel_id=1, source_target_pairs={{0,2},{1,3},{2,4},{3,5},{4,6},{5,7},{6,0},{7,1},{8,10},{9,11},{10,... | collective-permute-start | bytes 221360 | tf_op jit(solution)/shard_map/ppermute | solution.py:101
  555.6 258.1 %collective-permute-start.71 = (bf16[8,48,2,1536]{3,1,0,2:T(8,128)(2,1)}, bf16[8,48,2,1536]{3,1,0,2:T(8,128)(2,1)}, u32[]{:S(2)}, u32[]{:S(2)}) collective-permute-start(bf16[8,48,2,1536]{3,1,0,2:T(8,128)(2,1)} %bitcast.710), channel_id=1, source_target_pairs={{0,8},{8,0},{16,24},{24,16},{1,9},{9,1},{17,25},{25,17},{2,10},{10... | collective-permute-start | bytes 7077896 | tf_op jit(solution)/shard_map/ppermute | solution.py:33
  558.5 264.1 %collective-permute-start.79 = (bf16[8,192,2,384]{3,1,0,2:T(8,128)(2,1)}, bf16[8,192,2,384]{3,1,0,2:T(8,128)(2,1)}, u32[]{:S(2)}, u32[]{:S(2)}) collective-permute-start(bf16[8,192,2,384]{3,1,0,2:T(8,128)(2,1)} %bitcast.709), channel_id=1, source_target_pairs={{0,8},{8,0},{16,24},{24,16},{1,9},{9,1},{17,25},{25,17},{2,10},{10... | collective-permute-start | bytes 7077896 | tf_op jit(solution)/shard_map/ppermute | solution.py:33
  559.0 130.1 %collective-permute-start.92 = (f32[18446]{0:T(1024)S(1)}, f32[18446]{0:T(1024)}, u32[]{:S(2)}, u32[]{:S(2)}) collective-permute-start(f32[18446]{0:T(1024)S(1)} %collective-permute-done.91), channel_id=1, source_target_pairs={{0,2},{1,3},{2,4},{3,5},{4,6},{5,7},{6,0},{7,1},{8,10},{9,11},{10,... | collective-permute-start | bytes 221360 | tf_op jit(solution)/shard_map/ppermute | solution.py:101
  689.2 113.6 %collective-permute-start.38 = (bf16[2,384,768]{2,1,0:T(8,128)(2,1)}, bf16[2,384,768]{2,1,0:T(8,128)(2,1)}, u32[]{:S(2)}, u32[]{:S(2)}) collective-permute-start(bf16[2,384,768]{2,1,0:T(8,128)(2,1)} %fusion.100), channel_id=1, source_target_pairs={{0,8},{8,0},{16,24},{24,16},{1,9},{9,1},{17,25},{25,17},{2,10},{10... | collective-permute-start | bytes 3538952 | tf_op jit(solution)/shard_map/ppermute | solution.py:33
  746.6 73.0 %collective-permute-start.43 = (bf16[2,384,768]{2,1,0:T(8,128)(2,1)}, bf16[2,384,768]{2,1,0:T(8,128)(2,1)}, u32[]{:S(2)}, u32[]{:S(2)}) collective-permute-start(bf16[2,384,768]{2,1,0:T(8,128)(2,1)} %fusion.101), channel_id=1, source_target_pairs={{0,8},{8,0},{16,24},{24,16},{1,9},{9,1},{17,25},{25,17},{2,10},{10... | collective-permute-start | bytes 3538952 | tf_op jit(solution)/shard_map/ppermute | solution.py:33
  818.1 42.7 %collective-permute-start.72 = (bf16[8,48,1536]{2,1,0:T(8,128)(2,1)S(1)}, bf16[8,48,1536]{2,1,0:T(8,128)(2,1)S(1)}, u32[]{:S(2)}, u32[]{:S(2)}) collective-permute-start(bf16[8,48,1536]{2,1,0:T(8,128)(2,1)S(1)} %fusion.98), channel_id=1, source_target_pairs={{0,16},{8,24},{16,0},{24,8},{1,17},{9,25},{17,1},{25,9},{2,18},{10... | collective-permute-start | bytes 3538952 | tf_op jit(solution)/shard_map/ppermute | solution.py:33
  821.9 38.4 %collective-permute-start.44 = (bf16[384,768]{1,0:T(8,128)(2,1)S(1)}, bf16[384,768]{1,0:T(8,128)(2,1)S(1)}, u32[]{:S(2)}, u32[]{:S(2)}) collective-permute-start(bf16[384,768]{1,0:T(8,128)(2,1)S(1)} %fusion.111), channel_id=1, source_target_pairs={{0,16},{8,24},{16,0},{24,8},{1,17},{9,25},{17,1},{25,9},{2,18},{10... | collective-permute-start | bytes 1769480 | tf_op jit(solution)/shard_map/ppermute | solution.py:33
  825.1 59.8 %collective-permute-start.80 = (bf16[8,192,384]{2,1,0:T(8,128)(2,1)S(1)}, bf16[8,192,384]{2,1,0:T(8,128)(2,1)S(1)}, u32[]{:S(2)}, u32[]{:S(2)}) collective-permute-start(bf16[8,192,384]{2,1,0:T(8,128)(2,1)S(1)} %fusion.99), channel_id=1, source_target_pairs={{0,16},{8,24},{16,0},{24,8},{1,17},{9,25},{17,1},{25,9},{2,18},{10... | collective-permute-start | bytes 3538952 | tf_op jit(solution)/shard_map/ppermute | solution.py:33
  (212 other events, 1950.8 us)

commit v2 on v1

--- a/solution.py
+++ b/solution.py
@@ -1,6 +1,10 @@
+import functools
+
 import jax
 import jax.numpy as jnp
 from jax import lax
+from jax.experimental import pallas as pl
+from jax.experimental.pallas import tpu as pltpu
 from jax.sharding import PartitionSpec as P
 
 HEAD_DIM = 64
@@ -20,11 +24,11 @@
     return sorted(found)
 
 
-def ring_pairs(count, stride, radix):
+def ring_pairs(count, stride, radix, shift):
     pairs = []
     for source in range(count):
         digit = (source // stride) % radix
-        pairs.append((source, source + ((digit + 1) % radix - digit) * stride))
+        pairs.append((source, source + ((digit + shift) % radix - digit) * stride))
     return pairs
 
 
@@ -38,78 +42,70 @@
     return jnp.stack([jnp.where(bit == 0, value, other), jnp.where(bit == 0, other, value)], axis)
 
 
-def ring_gather(value):
-    count = lax.axis_size("fsdp")
-    index = lax.axis_index("fsdp")
-    total = value[None]
+def strides(count):
+    found = []
     stride = 1
     for radix in factors(count):
-        digit = (index // stride) % radix
-        pairs = ring_pairs(count, stride, radix)
-        current = total
-        parts = [total]
-        for _ in range(radix - 1):
-            current = lax.ppermute(current, "fsdp", pairs)
-            parts.append(current)
-        if radix == 2:
-            stacked = jnp.stack(
-                [jnp.where(digit == 0, parts[0], parts[1]), jnp.where(digit == 0, parts[1], parts[0])]
-            )
-        else:
-            stacked = jnp.zeros((radix,) + total.shape, total.dtype)
-            for step, part in enumerate(parts):
-                stacked = lax.dynamic_update_index_in_dim(
-                    stacked, part, lax.rem(digit - step + radix, radix), 0
-                )
-        total = stacked.reshape((radix * total.shape[0],) + value.shape)
+        found.append((radix, stride))
         stride *= radix
+    return found
+
+
+def digit_gather(total, radix, stride, axis):
+    count = lax.axis_size("fsdp")
+    digit = (lax.axis_index("fsdp") // stride) % radix
+    parts = [total] + [
+        lax.ppermute(total, "fsdp", ring_pairs(count, stride, radix, shift))
+        for shift in range(1, radix)
+    ]
+    if radix == 2:
+        return jnp.stack(
+            [jnp.where(digit == 0, parts[0], parts[1]), jnp.where(digit == 0, parts[1], parts[0])],
+            axis,
+        )
+    shape = total.shape[:axis] + (radix,) + total.shape[axis:]
+    stacked = jnp.zeros(shape, total.dtype)
+    for shift, part in enumerate(parts):
+        stacked = lax.dynamic_update_index_in_dim(
+            stacked, part, lax.rem(digit - shift + radix, radix), axis
+        )
+    return stacked
+
+
+def ring_gather(value):
+    total = value[None]
+    for radix, stride in reversed(strides(lax.axis_size("fsdp"))):
+        total = digit_gather(total, radix, stride, 1)
+        total = total.reshape((-1,) + value.shape)
     return total
 
 
+def digit_scatter(value, radix, stride, wire):
+    count = lax.axis_size("fsdp")
+    digit = (lax.axis_index("fsdp") // stride) % radix
+    view = value.reshape((value.shape[0] // radix, radix) + value.shape[1:])
+
+    def piece(offset):
+        return lax.dynamic_index_in_dim(view, lax.rem(digit + offset, radix), 1, keepdims=False)
+
+    total = piece(0)
+    for shift in range(1, radix):
+        moved = lax.ppermute(
+            piece(shift).astype(wire), "fsdp", ring_pairs(count, stride, radix, shift)
+        )
+        total = total + moved.astype(f32)
+    return total
+
+
 def ring_scatter(value, wire=bf16):
-    count = lax.axis_size("fsdp")
-    index = lax.axis_index("fsdp")
-    stride = 1
-    for radix in factors(count):
-        digit = (index // stride) % radix
-        pairs = ring_pairs(count, stride, radix)
-        view = value.reshape((value.shape[0] // radix, radix) + value.shape[1:])
-
-        def own(offset):
-            return lax.dynamic_index_in_dim(
-                view, lax.rem(digit + offset + 2 * radix, radix), 1, keepdims=False
-            )
-
-        current = own(-1)
-        for step in range(radix - 1):
-            moved = lax.ppermute(current.astype(wire), "fsdp", pairs)
-            current = own(-2 - step) + moved.astype(f32)
-        value = current
-        stride *= radix
+    for radix, stride in strides(lax.axis_size("fsdp")):
+        value = digit_scatter(value, radix, stride, wire)
     return value[0]
 
 
 def ring_sum(value):
-    count = lax.axis_size("fsdp")
-    stride = 1
-    for radix in factors(count):
-        pairs = ring_pairs(count, stride, radix)
-        index = (lax.axis_index("fsdp") // stride) % radix
-        current = value
-        parts = [value]
-        for _ in range(radix - 1):
-            current = lax.ppermute(current, "fsdp", pairs)
-            parts.append(current)
-        if radix == 2:
-            value = parts[0] + parts[1]
-        else:
-            stacked = jnp.zeros((radix,) + value.shape, value.dtype)
-            for step, part in enumerate(parts):
-                stacked = lax.dynamic_update_index_in_dim(
-                    stacked, part, lax.rem(index - step + radix, radix), 0
-                )
-            value = jnp.sum(stacked, axis=0)
-        stride *= radix
+    for radix, stride in strides(lax.axis_size("fsdp")):
+        value = jnp.sum(digit_gather(value, radix, stride, 0), axis=0)
     return value
 
 
@@ -141,21 +137,38 @@
     return pair_stack(gathered, 1, core, 1).reshape(-1, columns)
 
 
-def reduce_rows(grad, chip, core):
+def core_stage(grad, chip, core):
     rows, columns = grad.shape
     count = lax.axis_size("fsdp")
     half = rows // (2 * count)
     wide = columns // 2
-    view = grad.reshape(count, 2, half, 2, wide)
-    sent = lax.dynamic_index_in_dim(view, 1 - core, 1, keepdims=False).astype(bf16)
-    kept = lax.dynamic_index_in_dim(view, core, 1, keepdims=False)
-    kept = kept + swap(sent, 1).astype(f32)
-    sent = lax.dynamic_index_in_dim(kept, 1 - chip, 2, keepdims=False).astype(bf16)
-    kept = lax.dynamic_index_in_dim(kept, chip, 2, keepdims=False)
-    kept = kept + swap(sent, 2).astype(f32)
-    owned = ring_scatter(kept).astype(bf16)
-    both = pair_stack(owned, 2, chip, 1)
-    return pair_stack(both, 1, core, 0).reshape(2 * half, columns).astype(f32)
+    view = grad.reshape(count, 2, half, columns)
+    other = lax.dynamic_index_in_dim(view, 1 - core, 1, keepdims=False).astype(bf16)
+    total = lax.dynamic_index_in_dim(view, core, 1, keepdims=False) + swap(other, 1).astype(f32)
+    low, high = total[..., :wide], total[..., wide:]
+    return jnp.where(chip == 0, low, high), jnp.where(chip == 0, high, low).astype(bf16)
+
+
+def chip_stage(pair):
+    kept, sent = pair
+    return kept + swap(sent, 2).astype(f32)
+
+
+def collect(owned, chip, core):
+    both = pair_stack(owned.astype(bf16), 2, chip, 0)
+    both = jnp.concatenate([both[0], both[1]], axis=-1)
+    return pair_stack(both, 1, core, 0).reshape(-1, both.shape[-1]).astype(f32)
+
+
+def small_stages(value):
+    for radix, stride in strides(lax.axis_size("fsdp"))[:-1]:
+        value = digit_scatter(value, radix, stride, bf16)
+    return value
+
+
+def last_stage(value):
+    radix, stride = strides(lax.axis_size("fsdp"))[-1]
+    return digit_scatter(value, radix, stride, bf16)[0]
 
 
 def layer_norm(values, gain, shift):
@@ -209,81 +222,160 @@
     )
 
 
-def attention_forward(query, key, value, segments):
-    tokens, width = query.shape
+def nt(left, right, precision=None):
+    return lax.dot_general(left, right, (((1,), (1,)), ((), ())), precision=precision, preferred_element_type=f32)
+
+
+def forward_kernel(heads, query_ref, whole_ref, row_seg_ref, col_seg_ref, context_ref, log_ref):
+    width = heads * HEAD_DIM
+    rows = query_ref.shape[0]
+    same = col_seg_ref[...] == row_seg_ref[...]
+    lane = lax.broadcasted_iota(jnp.int32, (rows, 128), 1)
+    logs = jnp.zeros((rows, 128), f32)
+    pieces = []
+    for h in range(heads):
+        query = query_ref[:, h * HEAD_DIM : (h + 1) * HEAD_DIM] * jnp.asarray(HEAD_DIM ** (-0.5), bf16)
+        key = whole_ref[:, width + h * HEAD_DIM : width + (h + 1) * HEAD_DIM]
+        value = whole_ref[:, 2 * width + h * HEAD_DIM : 2 * width + (h + 1) * HEAD_DIM]
+        scores = jnp.where(same, nt(query, key), masked_value)
+        peak = jnp.max(scores, axis=1, keepdims=True)
+        exponent = jnp.exp(scores - peak)
+        total = jnp.sum(exponent, axis=1, keepdims=True)
+        context = jnp.dot(exponent.astype(bf16), value, preferred_element_type=f32)
+        pieces.append((context / total).astype(bf16))
+        logs = jnp.where(lane == h, peak + jnp.log(total), logs)
+    context_ref[...] = jnp.concatenate(pieces, axis=1)
+    log_ref[...] = jnp.transpose(logs)[:8]
+
+
+def attention_forward(projected, segments, rows=512):
+    tokens, triple = projected.shape
+    width = triple // 3
     heads = width // HEAD_DIM
-    scaling = HEAD_DIM ** (-0.5)
-    rows = min(512, tokens)
-    blocks = tokens // rows
-    key_all = key.reshape(tokens, heads, HEAD_DIM)
-    value_all = value.reshape(tokens, heads, HEAD_DIM)
-
-    def one_block(inputs):
-        query_part, segment_part = inputs
-        scores = jnp.einsum("qhd,khd->hqk", query_part, key_all, preferred_element_type=f32)
-        same = (segment_part[:, None] == segments[None, :])[None]
-        scores = jnp.where(same, scores * scaling, masked_value)
-        peak = jnp.max(scores, axis=-1, keepdims=True)
-        exponent = jnp.exp(scores - peak)
-        totals = jnp.sum(exponent, axis=-1, keepdims=True)
-        probs = (exponent / totals).astype(bf16)
-        context = jnp.einsum("hqk,khd->qhd", probs, value_all, preferred_element_type=f32)
-        return (context.astype(bf16), peak[:, :, 0] + jnp.log(totals[:, :, 0]))
-
-    contexts, logs = lax.map(
-        one_block,
-        (query.reshape(blocks, rows, heads, HEAD_DIM), segments.reshape(blocks, rows)),
-    )
-    return contexts.reshape(tokens, width), logs
-
-
-def attention_backward(query, key, value, segments, logs, grad_context):
-    tokens, width = query.shape
+    return pl.pallas_call(
+        functools.partial(forward_kernel, heads),
+        grid=(tokens // rows,),
+        in_specs=[
+            pl.BlockSpec((rows, triple), lambda i: (i, 0)),
+            pl.BlockSpec((tokens, triple), lambda i: (0, 0)),
+            pl.BlockSpec((1, tokens), lambda i: (0, 0)),
+            pl.BlockSpec((rows, 1), lambda i: (i, 0)),
+        ],
+        out_specs=[
+            pl.BlockSpec((rows, width), lambda i: (i, 0)),
+            pl.BlockSpec((8, rows), lambda i: (0, i)),
+        ],
+        out_shape=[
+            jax.ShapeDtypeStruct((tokens, width), bf16),
+            jax.ShapeDtypeStruct((8, tokens), f32),
+        ],
+        cost_estimate=pl.CostEstimate(flops=4 * tokens * tokens * 256 * heads, transcendentals=tokens * tokens * heads, bytes_accessed=10 * tokens * triple),
+        name="attention_forward",
+    )(projected, projected, segments[None, :], segments[:, None])
+
+
+def backward_kernel(heads, chunk, first, last, *refs):
+    width = heads * HEAD_DIM
+    part_ref, whole_ref, grad_ref, context_ref, log_ref, row_seg_ref, col_seg_ref = refs[:7]
+    if first:
+        query_ref, key_out, value_out, key_total, value_total = refs[7:]
+    else:
+        key_in, value_in, query_ref, key_out, value_out, key_total, value_total = refs[7:]
+    rows = grad_ref.shape[0]
+    tokens = whole_ref.shape[0]
+    step = pl.program_id(0)
+
+    @pl.when(step == 0)
+    def _():
+        if first:
+            key_total[...] = jnp.zeros_like(key_total)
+            value_total[...] = jnp.zeros_like(value_total)
+        else:
+            key_total[...] = key_in[...]
+            value_total[...] = value_in[...]
+
+    scale = HEAD_DIM ** (-0.5)
+    row_seg = row_seg_ref[...]
+    pieces = []
+    for h in range(heads):
+        cut = slice(h * HEAD_DIM, (h + 1) * HEAD_DIM)
+        query = part_ref[:, cut] * jnp.asarray(scale, bf16)
+        grad = grad_ref[:, cut]
+        inner = nt(
+            jnp.ones((8, HEAD_DIM), f32),
+            grad.astype(f32) * context_ref[:, cut].astype(f32),
+            highest,
+        )[:1]
+        log_row = log_ref[h : h + 1, :]
+        grad_query = jnp.zeros((rows, HEAD_DIM), f32)
+        for c in range(tokens // chunk):
+            span = slice(c * chunk, (c + 1) * chunk)
+            key = whole_ref[span, width + h * HEAD_DIM : width + (h + 1) * HEAD_DIM]
+            value = whole_ref[span, 2 * width + h * HEAD_DIM : 2 * width + (h + 1) * HEAD_DIM]
+            same = col_seg_ref[span, :] == row_seg
+            soft = jnp.exp(jnp.where(same, nt(key, query) - log_row, masked_value))
+            grad_scores = (soft * (nt(value, grad) - inner)).astype(bf16)
+            value_total[h, span, :] += jnp.dot(soft.astype(bf16), grad, preferred_element_type=f32)
+            key_total[h, span, :] += jnp.dot(grad_scores, query, preferred_element_type=f32)
+            grad_query += lax.dot_general(
+                grad_scores, key, (((0,), (0,)), ((), ())), preferred_element_type=f32
+            )
+        pieces.append((grad_query * scale).astype(bf16))
+    query_ref[...] = jnp.concatenate(pieces, axis=1)
+
+    @pl.when(step == pl.num_programs(0) - 1)
+    def _():
+        if last:
+            for total, out in ((key_total, key_out), (value_total, value_out)):
+                out[...] = jnp.concatenate([total[h].astype(bf16) for h in range(heads)], axis=1)
+        else:
+            key_out[...] = key_total[...]
+            value_out[...] = value_total[...]
+
+
+def attention_backward(
+    projected, segments, logs, context, grad_context, totals, start, calls, rows=256, chunk=768
+):
+    tokens, triple = projected.shape
+    width = triple // 3
     heads = width // HEAD_DIM
-    scaling = HEAD_DIM ** (-0.5)
-    rows = min(512, tokens)
-    blocks = tokens // rows
-    key_all = key.reshape(tokens, heads, HEAD_DIM)
-    value_all = value.reshape(tokens, heads, HEAD_DIM)
-
-    def one_block(carry, inputs):
-        query_part, segment_part, log_part, grad_part = inputs
-        scores = jnp.einsum("qhd,khd->hqk", query_part, key_all, preferred_element_type=f32)
-        same = (segment_part[:, None] == segments[None, :])[None]
-        soft = jnp.exp(jnp.where(same, scores * scaling, masked_value) - log_part[:, :, None])
-        grad_soft = jnp.einsum("qhd,khd->hqk", grad_part, value_all, preferred_element_type=f32)
-        inner = jnp.sum(soft * grad_soft, axis=-1, keepdims=True)
-        grad_scores = (soft * (grad_soft - inner)).astype(bf16)
-        grad_query = (
-            jnp.einsum("hqk,khd->qhd", grad_scores, key_all, preferred_element_type=f32) * scaling
-        )
-        grad_key = carry[0] + scaling * jnp.einsum(
-            "hqk,qhd->khd", grad_scores, query_part, preferred_element_type=f32
-        )
-        grad_value = carry[1] + jnp.einsum(
-            "hqk,qhd->khd", soft.astype(bf16), grad_part, preferred_element_type=f32
-        )
-        return ((grad_key, grad_value), grad_query.astype(bf16))
-
-    zeros = jnp.zeros((tokens, heads, HEAD_DIM), f32)
-    (grad_key, grad_value), grad_query = lax.scan(
-        one_block,
-        (zeros, zeros),
-        (
-            query.reshape(blocks, rows, heads, HEAD_DIM),
-            segments.reshape(blocks, rows),
-            logs,
-            grad_context.reshape(blocks, rows, heads, HEAD_DIM),
+    steps = tokens // rows // calls
+    base = start * steps
+    first, last = start == 0, start == calls - 1
+    whole = pl.BlockSpec((heads, tokens, HEAD_DIM), lambda i: (0, 0, 0))
+    in_specs = [
+        pl.BlockSpec((rows, triple), lambda i: (i + base, 0)),
+        pl.BlockSpec((tokens, triple), lambda i: (0, 0)),
+        pl.BlockSpec((rows, width), lambda i: (i + base, 0)),
+        pl.BlockSpec((rows, width), lambda i: (i + base, 0)),
+        pl.BlockSpec((8, rows), lambda i: (0, i + base)),
+        pl.BlockSpec((1, rows), lambda i: (0, i + base)),
+        pl.BlockSpec((tokens, 1), lambda i: (0, 0)),
+    ] + ([] if first else [whole] * 2)
+    if last:
+        end_spec = pl.BlockSpec((tokens, width), lambda i: (0, 0))
+        end_shape = jax.ShapeDtypeStruct((tokens, width), bf16)
+    else:
+        end_spec = whole
+        end_shape = jax.ShapeDtypeStruct((heads, tokens, HEAD_DIM), f32)
+    query, key, value = pl.pallas_call(
+        functools.partial(backward_kernel, heads, chunk, first, last),
+        grid=(steps,),
+        in_specs=in_specs,
+        out_specs=[pl.BlockSpec((rows, width), lambda i: (i, 0)), end_spec, end_spec],
+        out_shape=[jax.ShapeDtypeStruct((steps * rows, width), bf16), end_shape, end_shape],
+        scratch_shapes=[pltpu.VMEM((heads, tokens, HEAD_DIM), f32)] * 2,
+        cost_estimate=pl.CostEstimate(
+            flops=10 * tokens * tokens * 256 * heads // calls,
+            transcendentals=tokens * tokens * heads // calls,
+            bytes_accessed=14 * tokens * triple,
         ),
-    )
-    return jnp.concatenate(
-        [
-            grad_query.reshape(tokens, width),
-            grad_key.astype(bf16).reshape(tokens, width),
-            grad_value.astype(bf16).reshape(tokens, width),
-        ],
-        axis=1,
-    )
+        name="attention_backward",
+    )(
+        projected, projected, grad_context, context, logs,
+        segments[None, :], segments[:, None], *(() if first else totals),
+    )
+    return query, (key, value)
 
 
 def body(
@@ -334,33 +426,33 @@
         bias_out,
         gain_attn,
         shift_attn,
-        bias_up,
         bias_down,
         gain_ffn,
         shift_ffn,
-        bias_student,
-        w_student.reshape(-1),
-    )
-    small_all = ring_gather(jnp.concatenate(small_list))
-    full_small = []
-    start = 0
-    for part in small_list:
-        size = part.shape[0]
-        full_small.append(small_all[:, start : start + size].reshape(-1))
-        start += size
+    )
+    up_rows = bias_up.shape[0] // shard
+    student_size = bias_student.shape[0]
+    small_all = ring_gather(
+        jnp.concatenate(
+            [
+                jnp.stack(small_list),
+                bias_up.reshape(up_rows, shard),
+                jnp.pad(bias_student, (0, shard - student_size))[None],
+            ]
+        )
+    ).astype(f32)
     (
         full_bias_query,
         full_bias_value,
         full_bias_out,
         full_gain_attn,
         full_shift_attn,
-        full_bias_up,
         full_bias_down,
         full_gain_ffn,
         full_shift_ffn,
-        full_bias_student,
-    ) = [part.astype(f32) for part in full_small[:-1]]
-    full_student = full_small[-1].reshape(width, -1)
+    ) = [small_all[:, i].reshape(-1) for i in range(len(small_list))]
+    full_bias_up = small_all[:, len(small_list) : -1].reshape(-1)
+    full_bias_student = small_all[:, -1, :student_size].reshape(-1)
 
     own_qkv_shard = lax.dynamic_index_in_dim(
         w_qkv.reshape(shard, 3, seq_count, head_width), seq_index, 2, keepdims=False
@@ -380,9 +472,11 @@
         both = pair_stack(hidden[m], 2, chip, 0)
         full_hidden.append(pair_stack(both, 1, core, 1).reshape(group, width))
 
-    full_out = gather_rows(w_out, core)
-    full_up = gather_rows(w_up, core)
-    full_down = gather_rows(w_down, core)
+    own_qkv, full_hidden[0], *later = lax.optimization_barrier(
+        (own_qkv, full_hidden[0], w_out, w_up, w_down, w_student)
+    )
+    full_out, full_up, full_down = [gather_rows(part, core) for part in later[:3]]
+    full_student = ring_gather(later[3]).reshape(width, -1)
 
     segments = [segment_ids(slot_order[m, 0], lengths[m, 0]) for m in range(micro)]
 
@@ -390,11 +484,8 @@
     context_parts = []
     for m in range(micro):
         projected = (big_product(full_hidden[m], own_qkv) + own_bias).astype(bf16)
-        query = projected[:, :head_width]
-        key = projected[:, head_width : 2 * head_width]
-        value = projected[:, 2 * head_width :]
-        context_own, logs = attention_forward(query, key, value, segments[m])
-        saved.append((query, key, value, logs))
+        context_own, logs = attention_forward(projected, segments[m])
+        saved.append((projected, logs, context_own))
         view = context_own.reshape(seq_count, tokens, head_width)
         parts = []
         for mask in range(seq_count):
@@ -499,9 +590,14 @@
     )
     grad_context = right_product(grad_branch, out_turned).astype(bf16)
 
+    down = core_stage(grad_w_down, chip, core)
+    up = core_stage(grad_w_up, chip, core)
+    out = core_stage(grad_w_out, chip, core)
     grad_own_qkv = None
     grad_bias_own = None
     grad_inputs = []
+    calls = 3
+    slot = 0
     for m in range(micro):
         rows = grad_context[m * tokens : (m + 1) * tokens]
         parts = []
@@ -509,8 +605,36 @@
             part = rows[:, mask * head_width : (mask + 1) * head_width]
             parts.append(part if mask == 0 else swap(part, mask))
         grad_context_own = jnp.concatenate(by_seq(parts, chip, core), axis=0)
-        query, key, value, logs = saved[m]
-        grad_proj = attention_backward(query, key, value, segments[m], logs, grad_context_own)
+        projected, logs, context_own = saved[m]
+        totals = None
+        query_parts = []
+        for call in range(calls):
+            if slot == 0:
+                grad_context_own, down, up, out = lax.optimization_barrier(
+                    (grad_context_own, down, up, out)
+                )
+                down = chip_stage(down)
+            elif slot == 2:
+                grad_context_own, down = lax.optimization_barrier((grad_context_own, down))
+                up = chip_stage(up)
+                down = small_stages(down)
+            elif slot == 4:
+                grad_context_own, down, up = lax.optimization_barrier((grad_context_own, down, up))
+                out = chip_stage(out)
+                up = small_stages(up)
+                down = last_stage(down)
+            elif slot == 5:
+                grad_context_own, down, up, out = lax.optimization_barrier(
+                    (grad_context_own, down, up, out)
+                )
+                out = small_stages(out)
+                up = last_stage(up)
+            query_part, totals = attention_backward(
+                projected, segments[m], logs, context_own, grad_context_own, totals, call, calls
+            )
+            query_parts.append(query_part)
+            slot += 1
+        grad_proj = jnp.concatenate([jnp.concatenate(query_parts, axis=0), *totals], axis=1)
         bias_sum = jnp.sum(grad_proj.astype(f32), axis=0)
         weight_sum = left_product(full_hidden[m], grad_proj)
         grad_bias_own = bias_sum if grad_bias_own is None else grad_bias_own + bias_sum
@@ -524,9 +648,10 @@
         kept = kept + swap(sent, 2).astype(f32)
         grad_inputs.append(grad_res[m * tokens : (m + 1) * tokens] + kept)
 
-    out_w_down = reduce_rows(grad_w_down, chip, core)
-    out_w_up = reduce_rows(grad_w_up, chip, core)
-    out_w_out = reduce_rows(grad_w_out, chip, core)
+    out = last_stage(out)
+    out_w_down = collect(down, chip, core)
+    out_w_up = collect(up, chip, core)
+    out_w_out = collect(out, chip, core)
     owned_qkv = ring_scatter(grad_own_qkv.reshape(fsdp_count, shard, 3 * head_width)).astype(bf16)
     both = pair_stack(owned_qkv.reshape(shard, 3, head_width), 2, chip, 2)
     out_w_qkv = pair_stack(both, 1, core, 3).reshape(shard, 3 * width).astype(f32)

time: 949 us -> 657 us (0.69)
  matrix products: 259 us -> 103 us
  local copies, waits for them, and re-layouts: 209 us -> 76.9 us
  Pallas kernels: 0 us -> 112 us
  other arithmetic: 140 us -> 60.3 us
  waiting for transfers between devices: 250 us -> 191 us
  starting transfers between devices: 69 us -> 103 us
    dot_general x42 -> x0, matrix products: 157 us -> none  [the longest x12 55.9 us: one_block(): jnp.einsum('qhd,khd->hqk', query_part, key_all, preferred_element_type=f32)]
    pallas_call x0 -> x8, Pallas kernels: none -> 112 us  [the longest x6 78.1 us: attention_backward(): pl.pallas_call(functools.partial(backward_kernel, heads, chunk, first, la...]
    convert_element_type x29 -> x9, other arithmetic: 57.7 us -> 5.66 us  [the longest x3 3.02 us: collect(): return pair_stack(both, 1, core, 0).reshape(-1, both.shape[-1]).astype(f32)]
    ppermute x48 -> x52, waiting for transfers between devices: 165 us -> 119 us  [the longest x28 93.6 us: digit_gather(): lax.ppermute(total, 'fsdp', ring_pairs(count, stride, radix, shift))]
    dynamic_slice x22 -> x2, local copies, waits for them, and re-layouts: 37.6 us -> 0.2 us  [piece(): lax.dynamic_index_in_dim(view, lax.rem(digit + offset, radix), 1, keepdim...]
    reshape x13 -> x12, local copies, waits for them, and re-layouts: 38.6 us -> 1.53 us  [the longest x1 0.82 us: body(): bias_up.reshape(up_rows, shard)]
    ppermute x48 -> x52, starting transfers between devices: 44.4 us -> 74.7 us  [the longest x28 38.9 us: digit_gather(): lax.ppermute(total, 'fsdp', ring_pairs(count, stride, radix, shift))]
    reduce_sum x7 -> x2, other arithmetic: 17 us -> 0.2 us  [ring_sum(): value = jnp.sum(digit_gather(value, radix, stride, 0), axis=0)]
  transfers between devices with their start and end apart: 93 -> 97, of which waited for: 45 -> 34; matrix products, arithmetic and copies ran while one was open for 48% -> 21% of each run, Pallas kernels for 0% -> 17%
where the time goes in v2:
time: 657 us; the launch traced here: 649 us
  waiting for transfers between devices  191 us (29%)
  Pallas kernels  112 us (17%)
  starting transfers between devices  103 us (16%)
  matrix products  103 us (16%)
  local copies, waits for them, and re-layouts  76.9 us (12%)
  other arithmetic  60.3 us (9%)
    ppermute x28, waiting for transfers between devices, digit_gather(): lax.ppermute(total, 'fsdp', ring_pairs(count, stride, radix, shift))  93.6 us
    pallas_call x6, Pallas kernels, attention_backward(): pl.pallas_call(functools.partial(backward_kernel, heads, chunk, first, la...  78.1 us
    ppermute x45, waiting for transfers between devices, swap(): return lax.ppermute(value, 'seq', [(i, i ^ mask) for i in range(count)])  72 us
    dot_general x6, matrix products, big_product(): return jnp.dot(left, right, preferred_element_type=f32)  39.4 us
    ppermute x28, starting transfers between devices, digit_gather(): lax.ppermute(total, 'fsdp', ring_pairs(count, stride, radix, shift))  38.9 us
    ppermute x24, starting transfers between devices, digit_scatter(): lax.ppermute(piece(shift).astype(wire), 'fsdp', ring_pairs(count, stride,...  35.7 us
    pallas_call x2, Pallas kernels, attention_forward(): pl.pallas_call(functools.partial(forward_kernel, heads), grid=(tokens //...  33.6 us
    dot_general x6, matrix products, right_product(): lax.dot_general(left, right, (((1,), (1,)), ((), ())), preferred_element_...  32.1 us
  transfers between devices with their start and end apart: 97, of which 34 were waited for; matrix products, arithmetic and copies ran while one was open for 21% of the time, Pallas kernels for 17%

profile of v2, /device:TPU:8, one launch (start us, length us, event | category | flops | bytes accessed | tf_op | source)
XLA Modules:
  0.0 649.0 jit_solution(11745423366055174721)
XLA Ops:
  29.1 6.9 %collective-permute-done.4 = bf16[384,768]{1,0:T(8,128)(2,1)} collective-permute-done((bf16[384,768]{1,0:T(8,128)(2,1)S(1)}, bf16[384,768]{1,0:T(8,128)(2,1)}, u32[]{:S(2)}, u32[]{:S(2)}) %collective-permute-start.4) | collective-permute-done | bytes 589856 | tf_op jit(solution)/shard_map/ppermute | solution.py:37
  42.5 10.1 %collective-permute-done.3 = bf16[4,96,576]{2,1,0:T(8,128)(2,1)S(1)} collective-permute-done((bf16[4,96,576]{2,1,0:T(8,128)(2,1)S(1)}, bf16[4,96,576]{2,1,0:T(8,128)(2,1)S(1)}, u32[]{:S(2)}, u32[]{:S(2)}) %collective-permute-start.3) | collective-permute-done | bytes 442400 | tf_op jit(solution)/shard_map/ppermute | solution.py:58
  70.4 17.0 %attention_forward.3 = (bf16[1536,192]{1,0:T(8,128)(2,1)}, f32[8,1536]{1,0:T(8,128)}) custom-call(bf16[1536,576]{1,0:T(8,128)(2,1)} %add_convert_fusion.1.query_ref.whole_ref.refs_0_.refs_1_, bf16[1536,576]{1,0:T(8,128)(2,1)} %add_convert_fusion.1.query_ref.whole_ref.refs_0_.refs_1_, s32[1,1536]{1,0:T(1,128)} %broadcast_in_dim.184.row_seg_ref.refs_5_, ...), custom_call_target="tpu_custom_call" | custom-call | flops 7247757312 | bytes 8847360 | tf_op jit(solution)/shard_map/attention_forward/pallas_call | solution.py:255
  87.4 16.6 %attention_forward.2 = (bf16[1536,192]{1,0:T(8,128)(2,1)}, f32[8,1536]{1,0:T(8,128)}) custom-call(bf16[1536,576]{1,0:T(8,128)(2,1)} %add_convert_fusion.2.query_ref.whole_ref.refs_0_.refs_1_, bf16[1536,576]{1,0:T(8,128)(2,1)} %add_convert_fusion.2.query_ref.whole_ref.refs_0_.refs_1_, s32[1,1536]{1,0:T(1,128)} %broadcast_in_dim.182.row_seg_ref.refs_5_, ...), custom_call_target="tpu_custom_call" | custom-call | flops 7247757312 | bytes 8847360 | tf_op jit(solution)/shard_map/attention_forward/pallas_call | solution.py:255
  111.0 5.8 collective-permute-done.18
  130.3 14.3 %collective-permute-done.24 = bf16[1,48,3072]{2,1,0:T(8,128)(2,1)S(1)} collective-permute-done((bf16[1,48,3072]{2,1,0:T(8,128)(2,1)S(1)}, bf16[1,48,3072]{2,1,0:T(8,128)(2,1)S(1)}, u32[]{:S(2)}, u32[]{:S(2)}) %collective-permute-start.24) | collective-permute-done | bytes 294944 | tf_op jit(solution)/shard_map/ppermute | solution.py:58
  150.6 29.1 %collective-permute-done.21 = bf16[4,48,768]{2,1,0:T(8,128)(2,1)S(1)} collective-permute-done((bf16[4,48,768]{2,1,0:T(8,128)(2,1)S(1)}, bf16[4,48,768]{2,1,0:T(8,128)(2,1)S(1)}, u32[]{:S(2)}, u32[]{:S(2)}) %collective-permute-start.21) | collective-permute-done | bytes 294944 | tf_op jit(solution)/shard_map/ppermute | solution.py:58
  181.9 21.3 %collective-permute-done.26 = bf16[4,48,3072]{2,1,0:T(8,128)(2,1)S(1)} collective-permute-done((bf16[4,48,3072]{2,1,0:T(8,128)(2,1)S(1)}, bf16[4,48,3072]{2,1,0:T(8,128)(2,1)S(1)}, u32[]{:S(2)}, u32[]{:S(2)}) %collective-permute-start.26) | collective-permute-done | bytes 1179680 | tf_op jit(solution)/shard_map/ppermute | solution.py:58
  220.4 26.8 %multiply_convert_fusion = (bf16[768,3072]{1,0:T(8,128)(2,1)S(1)}, f32[768,3072]{1,0:T(8,128)}, f32[768,3072]{1,0:T(8,128)}) fusion(f32[3072]{0:T(1024)S(1)} %copy-done.71, bf16[768,3072]{1,0:T(8,128)(2,1)S(1)} %bitcast.420, f32[768,768]{1,0:T(8,128)S(1)} %get-tuple-element.370, f32[768]{0:T(1024)S(1)} %add.598, f32[768]{0:T(1024)S(1)} %mul.279, ...), kind=kOutput, calls=%fused_computation.4 | convolution fusion | flops 3782541312 | bytes 30695424 | tf_op jit(solution)/shard_map/dot_general | solution.py:203
  271.2 13.7 %convert_reduce_fusion = (f32[3072]{0:T(1024)}, bf16[768,3072]{1,0:T(8,128)(2,1)}) fusion(f32[768,3072]{1,0:T(8,128)} %get-tuple-element.244, f32[768,3072]{1,0:T(8,128)} %get-tuple-element.371, f32[3072]{0:T(1024)S(1)} %copy-done.71, bf16[768,768]{1,0:T(8,128)(2,1)S(1)} %get-tuple-element.228, bf16[3072,768]{1,0:T(8,128)(2,1)S(1)} %bitcast.419), kind=kOutput, calls=%fused_computation.2 | convolution fusion | flops 3663983616 | bytes 29515776 | tf_op jit(solution)/shard_map/dot_general | solution.py:211
  284.9 6.9 %multiply_reduce_fusion.1 = (f32[768]{0:T(1024)S(1)}, f32[768]{0:T(1024)S(1)}, f32[768]{0:T(1024)S(1)}, f32[768,768]{1,0:T(8,128)S(1)}) fusion(f32[768,768]{1,0:T(8,128)S(1)} %copy-done.4, f32[768]{0:T(1024)S(1)} %fusion.49, f32[768]{0:T(1024)S(1)} %broadcast_multiply_fusion.1, f32[768]{0:T(1024)S(1)} %mul.279, bf16[768,3072]{1,0:T(8,128)(2,1)} %get-tuple-element.230, ...), kind=kOutput, calls=%fused_computation.46 | convolution fusion | flops 3629774592 | bytes 16536576 | tf_op jit(solution)/shard_map/dot_general | solution.py:211
  296.3 12.3 %fusion.87 = f32[3072,768]{1,0:T(8,128)} fusion(bf16[768,3072]{1,0:T(8,128)(2,1)} %copy-done.93, bf16[768,768]{1,0:T(8,128)(2,1)S(1)} %copy-done.25), kind=kOutput, calls=%fused_computation.399 | convolution fusion | flops 3623878656 | bytes 15335424 | tf_op jit(solution)/shard_map/dot_general | solution.py:207
  362.1 5.9 collective-permute-done.50
  384.3 12.6 %attention_backward.9 = (bf16[512,192]{1,0:T(8,128)(2,1)}, f32[3,1536,64]{2,1,0:T(8,128)}, f32[3,1536,64]{2,1,0:T(8,128)}) custom-call(bf16[1536,576]{1,0:T(8,128)(2,1)} %add_convert_fusion.1.query_ref.whole_ref.refs_0_.refs_1_, bf16[1536,576]{1,0:T(8,128)(2,1)} %add_convert_fusion.1.query_ref.whole_ref.refs_0_.refs_1_, ...), custom_call_target="tpu_custom_call" | custom-call | flops 6039797760 | bytes 12386304 | tf_op jit(solution)/shard_map/attention_backward/pallas_call | solution.py:361
  414.0 12.1 %attention_backward.6 = (bf16[512,192]{1,0:T(8,128)(2,1)}, f32[3,1536,64]{2,1,0:T(8,128)}, f32[3,1536,64]{2,1,0:T(8,128)}) custom-call(bf16[1536,576]{1,0:T(8,128)(2,1)} %add_convert_fusion.2.query_ref.whole_ref.refs_0_.refs_1_, bf16[1536,576]{1,0:T(8,128)(2,1)} %add_convert_fusion.2.query_ref.whole_ref.refs_0_.refs_1_, ...), custom_call_target="tpu_custom_call" | custom-call | flops 6039797760 | bytes 12386304 | tf_op jit(solution)/shard_map/attention_backward/pallas_call | solution.py:361
  426.1 13.8 %attention_backward.7 = (bf16[512,192]{1,0:T(8,128)(2,1)}, f32[3,1536,64]{2,1,0:T(8,128)}, f32[3,1536,64]{2,1,0:T(8,128)}) custom-call(bf16[1536,576]{1,0:T(8,128)(2,1)} %add_convert_fusion.2.query_ref.whole_ref.refs_0_.refs_1_, bf16[1536,576]{1,0:T(8,128)(2,1)} %add_convert_fusion.2.query_ref.whole_ref.refs_0_.refs_1_, ...), custom_call_target="tpu_custom_call" | custom-call | flops 6039797760 | bytes 12386304 | tf_op jit(solution)/shard_map/attention_backward/pallas_call | solution.py:361
  441.8 29.2 %collective-permute-done.45 = bf16[8,192,384]{2,1,0:T(8,128)(2,1)} collective-permute-done((bf16[8,192,384]{2,1,0:T(8,128)(2,1)}, bf16[8,192,384]{2,1,0:T(8,128)(2,1)}, u32[]{:S(2)}, u32[]{:S(2)}) %collective-permute-start.45) | collective-permute-done | bytes 1179680 | tf_op jit(solution)/shard_map/ppermute | solution.py:37
  476.0 12.6 %attention_backward.8 = (bf16[512,192]{1,0:T(8,128)(2,1)}, bf16[1536,192]{1,0:T(8,128)(2,1)}, bf16[1536,192]{1,0:T(8,128)(2,1)}) custom-call(bf16[1536,576]{1,0:T(8,128)(2,1)} %add_convert_fusion.2.query_ref.whole_ref.refs_0_.refs_1_, bf16[1536,576]{1,0:T(8,128)(2,1)} %add_convert_fusion.2.query_ref.whole_ref.refs_0_.refs_1_, ...), custom_call_target="tpu_custom_call" | custom-call | flops 6039797760 | bytes 12386304 | tf_op jit(solution)/shard_map/attention_backward/pallas_call | solution.py:361
  508.3 14.2 %attention_backward.10 = (bf16[512,192]{1,0:T(8,128)(2,1)}, f32[3,1536,64]{2,1,0:T(8,128)}, f32[3,1536,64]{2,1,0:T(8,128)}) custom-call(bf16[1536,576]{1,0:T(8,128)(2,1)} %add_convert_fusion.1.query_ref.whole_ref.refs_0_.refs_1_, bf16[1536,576]{1,0:T(8,128)(2,1)} %add_convert_fusion.1.query_ref.whole_ref.refs_0_.refs_1_, ...), custom_call_target="tpu_custom_call" | custom-call | flops 6039797760 | bytes 12386304 | tf_op jit(solution)/shard_map/attention_backward/pallas_call | solution.py:361
  529.6 12.8 %attention_backward.11 = (bf16[512,192]{1,0:T(8,128)(2,1)}, bf16[1536,192]{1,0:T(8,128)(2,1)}, bf16[1536,192]{1,0:T(8,128)(2,1)}) custom-call(bf16[1536,576]{1,0:T(8,128)(2,1)} %add_convert_fusion.1.query_ref.whole_ref.refs_0_.refs_1_, bf16[1536,576]{1,0:T(8,128)(2,1)} %add_convert_fusion.1.query_ref.whole_ref.refs_0_.refs_1_, ...), custom_call_target="tpu_custom_call" | custom-call | flops 6039797760 | bytes 12386304 | tf_op jit(solution)/shard_map/attention_backward/pallas_call | solution.py:361
  544.9 5.4 fusion.71
  551.7 5.5 convolution_add_fusion
  611.2 5.5 collective-permute-done.62
  638.5 6.5 %collective-permute-done.59 = bf16[384,768]{1,0:T(8,128)(2,1)S(1)} collective-permute-done((bf16[384,768]{1,0:T(8,128)(2,1)}, bf16[384,768]{1,0:T(8,128)(2,1)S(1)}, u32[]{:S(2)}, u32[]{:S(2)}) %collective-permute-start.59) | collective-permute-done | bytes 589856 | tf_op jit(solution)/shard_map/ppermute | solution.py:37
  (710 shorter events, 328.3 us)
Async XLA Ops:
  10.5 25.5 %collective-permute-start.4 = (bf16[384,768]{1,0:T(8,128)(2,1)S(1)}, bf16[384,768]{1,0:T(8,128)(2,1)}, u32[]{:S(2)}, u32[]{:S(2)}) collective-permute-start(bf16[384,768]{1,0:T(8,128)(2,1)S(1)} %get-tuple-element.294), channel_id=1, source_target_pairs={{0,16},{8,24},{16,0},{24,8},{1,17},{9,25},{17,1},{25,9},{2,18},{10... | collective-permute-start | bytes 1769480 | tf_op jit(solution)/shard_map/ppermute | solution.py:37
  55.4 50.4 %collective-permute-start.33 = (bf16[1,96,128]{2,1,0:T(8,128)(2,1)S(1)}, bf16[1,96,128]{2,1,0:T(8,128)(2,1)S(1)}, u32[]{:S(2)}, u32[]{:S(2)}) collective-permute-start(bf16[1,96,128]{2,1,0:T(8,128)(2,1)S(1)} %bitcast.460), channel_id=1, source_target_pairs={{0,2},{1,3},{2,4},{3,5},{4,6},{5,7},{6,0},{7,1},{8,10},{9,11},{10,... | collective-permute-start | bytes 73736 | tf_op jit(solution)/shard_map/ppermute | solution.py:58
  55.7 50.2 %collective-permute-start.34 = (bf16[1,96,128]{2,1,0:T(8,128)(2,1)S(1)}, bf16[1,96,128]{2,1,0:T(8,128)(2,1)S(1)}, u32[]{:S(2)}, u32[]{:S(2)}) collective-permute-start(bf16[1,96,128]{2,1,0:T(8,128)(2,1)S(1)} %bitcast.461), channel_id=1, source_target_pairs={{0,4},{1,5},{2,6},{3,7},{4,0},{5,1},{6,2},{7,3},{8,12},{9,13},{10,... | collective-permute-start | bytes 73736 | tf_op jit(solution)/shard_map/ppermute | solution.py:58
  59.1 48.9 %collective-permute-start.35 = (bf16[1,96,128]{2,1,0:T(8,128)(2,1)S(1)}, bf16[1,96,128]{2,1,0:T(8,128)(2,1)S(1)}, u32[]{:S(2)}, u32[]{:S(2)}) collective-permute-start(bf16[1,96,128]{2,1,0:T(8,128)(2,1)S(1)} %bitcast.462), channel_id=1, source_target_pairs={{0,6},{1,7},{2,0},{3,1},{4,2},{5,3},{6,4},{7,5},{8,14},{9,15},{10,... | collective-permute-start | bytes 73736 | tf_op jit(solution)/shard_map/ppermute | solution.py:58
  59.2 63.2 %collective-permute-start.28 = (bf16[1,192,768]{2,1,0:T(8,128)(2,1)S(1)}, bf16[1,192,768]{2,1,0:T(8,128)(2,1)S(1)}, u32[]{:S(2)}, u32[]{:S(2)}) collective-permute-start(bf16[1,192,768]{2,1,0:T(8,128)(2,1)S(1)} %get-tuple-element.242), channel_id=1, source_target_pairs={{0,2},{1,3},{2,4},{3,5},{4,6},{5,7},{6,0},{7,1},{8,10},{9,11},{10,... | collective-permute-start | bytes 884744 | tf_op jit(solution)/shard_map/ppermute | solution.py:58
  61.4 63.3 %collective-permute-start.29 = (bf16[1,192,768]{2,1,0:T(8,128)(2,1)S(1)}, bf16[1,192,768]{2,1,0:T(8,128)(2,1)S(1)}, u32[]{:S(2)}, u32[]{:S(2)}) collective-permute-start(bf16[1,192,768]{2,1,0:T(8,128)(2,1)S(1)} %get-tuple-element.242), channel_id=1, source_target_pairs={{0,4},{1,5},{2,6},{3,7},{4,0},{5,1},{6,2},{7,3},{8,12},{9,13},{10,... | collective-permute-start | bytes 884744 | tf_op jit(solution)/shard_map/ppermute | solution.py:58
  122.4 26.1 %collective-permute-start.25 = (bf16[1,48,3072]{2,1,0:T(8,128)(2,1)S(1)}, bf16[1,48,3072]{2,1,0:T(8,128)(2,1)S(1)}, u32[]{:S(2)}, u32[]{:S(2)}) collective-permute-start(bf16[1,48,3072]{2,1,0:T(8,128)(2,1)S(1)} %get-tuple-element.246), channel_id=1, source_target_pairs={{0,6},{1,7},{2,0},{3,1},{4,2},{5,3},{6,4},{7,5},{8,14},{9,15},{10,... | collective-permute-start | bytes 884744 | tf_op jit(solution)/shard_map/ppermute | solution.py:58
  124.7 79.7 %collective-permute-start.15 = (bf16[384,192]{1,0:T(8,128)(2,1)S(1)}, bf16[384,192]{1,0:T(8,128)(2,1)S(1)}, u32[]{:S(2)}, u32[]{:S(2)}) collective-permute-start(bf16[384,192]{1,0:T(8,128)(2,1)S(1)} %get-tuple-element.313), channel_id=1, source_target_pairs={{0,8},{8,0},{16,24},{24,16},{1,9},{9,1},{17,25},{25,17},{2,10},{10... | collective-permute-start | bytes 442376 | tf_op jit(solution)/shard_map/ppermute | solution.py:37
  124.8 79.7 %collective-permute-start.16 = (bf16[384,192]{1,0:T(8,128)(2,1)S(1)}, bf16[384,192]{1,0:T(8,128)(2,1)S(1)}, u32[]{:S(2)}, u32[]{:S(2)}) collective-permute-start(bf16[384,192]{1,0:T(8,128)(2,1)S(1)} %get-tuple-element.312), channel_id=1, source_target_pairs={{0,16},{8,24},{16,0},{24,8},{1,17},{9,25},{17,1},{25,9},{2,18},{10... | collective-permute-start | bytes 442376 | tf_op jit(solution)/shard_map/ppermute | solution.py:37
  144.6 35.3 %collective-permute-start.31 = (bf16[4,192,768]{2,1,0:T(8,128)(2,1)S(1)}, bf16[4,192,768]{2,1,0:T(8,128)(2,1)S(1)}, u32[]{:S(2)}, u32[]{:S(2)}) collective-permute-start(bf16[4,192,768]{2,1,0:T(8,128)(2,1)S(1)} %constant_dynamic-update-slice_fusion.4), channel_id=1, source_target_pairs={{0,1},{1,0},{2,3},{3,2},{4,5},{5,4},{6,7},{7,6},{8,9},{9,8},{10,11... | collective-permute-start | bytes 3538952 | tf_op jit(solution)/shard_map/ppermute | solution.py:58
  148.5 31.3 %collective-permute-start.21 = (bf16[4,48,768]{2,1,0:T(8,128)(2,1)S(1)}, bf16[4,48,768]{2,1,0:T(8,128)(2,1)S(1)}, u32[]{:S(2)}, u32[]{:S(2)}) collective-permute-start(bf16[4,48,768]{2,1,0:T(8,128)(2,1)S(1)} %constant_dynamic-update-slice_fusion.12), channel_id=1, source_target_pairs={{0,1},{1,0},{2,3},{3,2},{4,5},{5,4},{6,7},{7,6},{8,9},{9,8},{10,11... | collective-permute-start | bytes 884744 | tf_op jit(solution)/shard_map/ppermute | solution.py:58
  150.0 53.2 %collective-permute-start.26 = (bf16[4,48,3072]{2,1,0:T(8,128)(2,1)S(1)}, bf16[4,48,3072]{2,1,0:T(8,128)(2,1)S(1)}, u32[]{:S(2)}, u32[]{:S(2)}) collective-permute-start(bf16[4,48,3072]{2,1,0:T(8,128)(2,1)S(1)} %constant_dynamic-update-slice_fusion.8), channel_id=1, source_target_pairs={{0,1},{1,0},{2,3},{3,2},{4,5},{5,4},{6,7},{7,6},{8,9},{9,8},{10,11... | collective-permute-start | bytes 3538952 | tf_op jit(solution)/shard_map/ppermute | solution.py:58
  179.7 26.3 %collective-permute-start.17 = (bf16[384,192]{1,0:T(8,128)(2,1)S(1)}, bf16[384,192]{1,0:T(8,128)(2,1)S(1)}, u32[]{:S(2)}, u32[]{:S(2)}) collective-permute-start(bf16[384,192]{1,0:T(8,128)(2,1)S(1)} %get-tuple-element.311), channel_id=1, source_target_pairs={{0,24},{8,16},{16,8},{24,0},{1,25},{9,17},{17,9},{25,1},{2,26},{10... | collective-permute-start | bytes 442376 | tf_op jit(solution)/shard_map/ppermute | solution.py:37
  179.9 23.8 %collective-permute-start.22 = (bf16[8,48,768]{2,1,0:T(8,128)(2,1)S(1)}, bf16[8,48,768]{2,1,0:T(8,128)(2,1)S(1)}, u32[]{:S(2)}, u32[]{:S(2)}) collective-permute-start(bf16[8,48,768]{2,1,0:T(8,128)(2,1)S(1)} %bitcast.429), channel_id=1, source_target_pairs={{0,8},{8,0},{16,24},{24,16},{1,9},{9,1},{17,25},{25,17},{2,10},{10... | collective-permute-start | bytes 1769480 | tf_op jit(solution)/shard_map/ppermute | solution.py:37
  316.0 83.7 %collective-permute-start.44 = (bf16[8,48,768]{2,1,0:T(8,128)(2,1)}, bf16[8,48,768]{2,1,0:T(8,128)(2,1)}, u32[]{:S(2)}, u32[]{:S(2)}) collective-permute-start(bf16[8,48,768]{2,1,0:T(8,128)(2,1)} %fusion.19), channel_id=1, source_target_pairs={{0,8},{8,0},{16,24},{24,16},{1,9},{9,1},{17,25},{25,17},{2,10},{10... | collective-permute-start | bytes 1769480 | tf_op jit(solution)/shard_map/ppermute | solution.py:37
  318.4 82.7 %collective-permute-start.43 = (bf16[8,48,3072]{2,1,0:T(8,128)(2,1)}, bf16[8,48,3072]{2,1,0:T(8,128)(2,1)}, u32[]{:S(2)}, u32[]{:S(2)}) collective-permute-start(bf16[8,48,3072]{2,1,0:T(8,128)(2,1)} %fusion.6), channel_id=1, source_target_pairs={{0,8},{8,0},{16,24},{24,16},{1,9},{9,1},{17,25},{25,17},{2,10},{10... | collective-permute-start | bytes 7077896 | tf_op jit(solution)/shard_map/ppermute | solution.py:37
  410.9 29.0 %collective-permute-start.57 = (bf16[8,48,384]{2,1,0:T(8,128)(2,1)S(1)}, bf16[8,48,384]{2,1,0:T(8,128)(2,1)}, u32[]{:S(2)}, u32[]{:S(2)}) collective-permute-start(bf16[8,48,384]{2,1,0:T(8,128)(2,1)S(1)} %select_convert_fusion.2), channel_id=1, source_target_pairs={{0,16},{8,24},{16,0},{24,8},{1,17},{9,25},{17,1},{25,9},{2,18},{10... | collective-permute-start | bytes 884744 | tf_op jit(solution)/shard_map/ppermute | solution.py:37
  411.9 84.4 %collective-permute-start.52 = (bf16[8,48,1536]{2,1,0:T(8,128)(2,1)}, bf16[8,48,1536]{2,1,0:T(8,128)(2,1)}, u32[]{:S(2)}, u32[]{:S(2)}) collective-permute-start(bf16[8,48,1536]{2,1,0:T(8,128)(2,1)} %select_convert_fusion), channel_id=1, source_target_pairs={{0,16},{8,24},{16,0},{24,8},{1,17},{9,25},{17,1},{25,9},{2,18},{10... | collective-permute-start | bytes 3538952 | tf_op jit(solution)/shard_map/ppermute | solution.py:37
  412.9 58.0 %collective-permute-start.45 = (bf16[8,192,384]{2,1,0:T(8,128)(2,1)}, bf16[8,192,384]{2,1,0:T(8,128)(2,1)}, u32[]{:S(2)}, u32[]{:S(2)}) collective-permute-start(bf16[8,192,384]{2,1,0:T(8,128)(2,1)} %select_convert_fusion.1), channel_id=1, source_target_pairs={{0,16},{8,24},{16,0},{24,8},{1,17},{9,25},{17,1},{25,9},{2,18},{10... | collective-permute-start | bytes 3538952 | tf_op jit(solution)/shard_map/ppermute | solution.py:37
  475.4 26.1 %collective-permute-start.51 = (bf16[4,192,384]{2,1,0:T(8,128)(2,1)}, bf16[4,192,384]{2,1,0:T(8,128)(2,1)}, u32[]{:S(2)}, u32[]{:S(2)}) collective-permute-start(bf16[4,192,384]{2,1,0:T(8,128)(2,1)} %fusion.22), channel_id=1, source_target_pairs={{0,1},{1,0},{2,3},{3,2},{4,5},{5,4},{6,7},{7,6},{8,9},{9,8},{10,11... | collective-permute-start | bytes 1769480 | tf_op jit(solution)/shard_map/ppermute | solution.py:93
  493.4 29.2 %collective-permute-start.46 = (bf16[2,384,768]{2,1,0:T(8,128)(2,1)}, bf16[2,384,768]{2,1,0:T(8,128)(2,1)}, u32[]{:S(2)}, u32[]{:S(2)}) collective-permute-start(bf16[2,384,768]{2,1,0:T(8,128)(2,1)} %fusion.10), channel_id=1, source_target_pairs={{0,8},{8,0},{16,24},{24,16},{1,9},{9,1},{17,25},{25,17},{2,10},{10... | collective-permute-start | bytes 3538952 | tf_op jit(solution)/shard_map/ppermute | solution.py:37
  502.8 25.6 %collective-permute-start.56 = (bf16[4,48,1536]{2,1,0:T(8,128)(2,1)S(1)}, bf16[4,48,1536]{2,1,0:T(8,128)(2,1)}, u32[]{:S(2)}, u32[]{:S(2)}) collective-permute-start(bf16[4,48,1536]{2,1,0:T(8,128)(2,1)S(1)} %fusion.23), channel_id=1, source_target_pairs={{0,1},{1,0},{2,3},{3,2},{4,5},{5,4},{6,7},{7,6},{8,9},{9,8},{10,11... | collective-permute-start | bytes 1769480 | tf_op jit(solution)/shard_map/ppermute | solution.py:93
  527.4 111.1 %collective-permute-start.47 = (bf16[384,768]{1,0:T(8,128)(2,1)}, bf16[384,768]{1,0:T(8,128)(2,1)}, u32[]{:S(2)}, u32[]{:S(2)}) collective-permute-start(bf16[384,768]{1,0:T(8,128)(2,1)} %fusion.20), channel_id=1, source_target_pairs={{0,16},{8,24},{16,0},{24,8},{1,17},{9,25},{17,1},{25,9},{2,18},{10... | collective-permute-start | bytes 1769480 | tf_op jit(solution)/shard_map/ppermute | solution.py:37
  550.3 33.9 %collective-permute-start.89 = (bf16[192,384]{1,0:T(8,128)(2,1)S(1)}, bf16[192,384]{1,0:T(8,128)(2,1)S(1)}, u32[]{:S(2)}, u32[]{:S(2)}) collective-permute-start(bf16[192,384]{1,0:T(8,128)(2,1)S(1)} %add_bitcast_fusion), channel_id=1, source_target_pairs={{0,16},{8,24},{16,0},{24,8},{1,17},{9,25},{17,1},{25,9},{2,18},{10... | collective-permute-start | bytes 442376 | tf_op jit(solution)/shard_map/ppermute | solution.py:37
  (174 other events, 1907.7 us)

commit v3 on v2

--- a/solution.py
+++ b/solution.py
@@ -472,11 +472,9 @@
         both = pair_stack(hidden[m], 2, chip, 0)
         full_hidden.append(pair_stack(both, 1, core, 1).reshape(group, width))
 
-    own_qkv, full_hidden[0], *later = lax.optimization_barrier(
-        (own_qkv, full_hidden[0], w_out, w_up, w_down, w_student)
-    )
-    full_out, full_up, full_down = [gather_rows(part, core) for part in later[:3]]
-    full_student = ring_gather(later[3]).reshape(width, -1)
+    own_qkv, student_shard = lax.optimization_barrier((own_qkv, w_student))
+    full_out, full_up, full_down = [gather_rows(part, core) for part in (w_out, w_up, w_down)]
+    full_student = ring_gather(student_shard).reshape(width, -1)
 
     segments = [segment_ids(slot_order[m, 0], lengths[m, 0]) for m in range(micro)]
 

time: 657 us -> 665 us (1.012)
  waiting for transfers between devices: 191 us -> 169 us
  local copies, waits for them, and re-layouts: 76.9 us -> 95.8 us
  other arithmetic: 60.3 us -> 69.3 us
    dynamic_update_slice x28, local copies, waits for them, and re-layouts: 8.57 us -> 21.3 us  [digit_gather(): lax.dynamic_update_index_in_dim(stacked, part, lax.rem(digit - shift + ra...]
    ppermute x28, waiting for transfers between devices: 93.6 us -> 83.2 us  [digit_gather(): lax.ppermute(total, 'fsdp', ring_pairs(count, stride, radix, shift))]
    ppermute x45, waiting for transfers between devices: 72 us -> 64.8 us  [swap(): return lax.ppermute(value, 'seq', [(i, i ^ mask) for i in range(count)])]
    unnamed x212 -> x182, local copies, waits for them, and re-layouts: 12.5 us -> 14.2 us
  transfers between devices with their start and end apart: 97 -> 97, of which waited for: 34 -> 32; matrix products, arithmetic and copies ran while one was open for 21% -> 25% of each run, Pallas kernels for 17% -> 17%
where the time goes in v3:
time: 665 us; the launch traced here: 655 us
  waiting for transfers between devices  169 us (25%)
  Pallas kernels  112 us (17%)
  matrix products  105 us (16%)
  starting transfers between devices  102 us (15%)
  local copies, waits for them, and re-layouts  95.8 us (14%)
  other arithmetic  69.3 us (10%)
    ppermute x28, waiting for transfers between devices, digit_gather(): lax.ppermute(total, 'fsdp', ring_pairs(count, stride, radix, shift))  83.2 us
    pallas_call x6, Pallas kernels, attention_backward(): pl.pallas_call(functools.partial(backward_kernel, heads, chunk, first, la...  77.8 us
    ppermute x45, waiting for transfers between devices, swap(): return lax.ppermute(value, 'seq', [(i, i ^ mask) for i in range(count)])  64.8 us
    dot_general x6, matrix products, big_product(): return jnp.dot(left, right, preferred_element_type=f32)  40.6 us
    ppermute x24, starting transfers between devices, digit_scatter(): lax.ppermute(piece(shift).astype(wire), 'fsdp', ring_pairs(count, stride,...  39.7 us
    ppermute x28, starting transfers between devices, digit_gather(): lax.ppermute(total, 'fsdp', ring_pairs(count, stride, radix, shift))  34.7 us
    pallas_call x2, Pallas kernels, attention_forward(): pl.pallas_call(functools.partial(forward_kernel, heads), grid=(tokens //...  33.9 us
    dot_general x6, matrix products, left_product(): lax.dot_general(left, right, (((0,), (0,)), ((), ())), preferred_element_...  30.9 us
  transfers between devices with their start and end apart: 97, of which 32 were waited for; matrix products, arithmetic and copies ran while one was open for 25% of the time, Pallas kernels for 17%

profile of v3, /device:TPU:8, one launch (start us, length us, event | category | flops | bytes accessed | tf_op | source)
XLA Modules:
  0.0 655.3 jit_solution(13063568248416681827)
XLA Ops:
  35.3 10.4 %collective-permute-done.20 = bf16[1,48,768]{2,1,0:T(8,128)(2,1)S(1)} collective-permute-done((bf16[1,48,768]{2,1,0:T(8,128)(2,1)}, bf16[1,48,768]{2,1,0:T(8,128)(2,1)S(1)}, u32[]{:S(2)}, u32[]{:S(2)}) %collective-permute-start.20) | collective-permute-done | bytes 73760 | tf_op jit(solution)/shard_map/ppermute | solution.py:58
  50.6 4.7 collective-permute-start.24
  58.5 16.2 %collective-permute-done.29 = bf16[1,192,768]{2,1,0:T(8,128)(2,1)} collective-permute-done((bf16[1,192,768]{2,1,0:T(8,128)(2,1)}, bf16[1,192,768]{2,1,0:T(8,128)(2,1)}, u32[]{:S(2)}, u32[]{:S(2)}) %collective-permute-start.29) | collective-permute-done | bytes 294944 | tf_op jit(solution)/shard_map/ppermute | solution.py:58
  91.5 10.0 %collective-permute-done.5 = bf16[4,96,576]{2,1,0:T(8,128)(2,1)S(1)} collective-permute-done((bf16[4,96,576]{2,1,0:T(8,128)(2,1)S(1)}, bf16[4,96,576]{2,1,0:T(8,128)(2,1)S(1)}, u32[]{:S(2)}, u32[]{:S(2)}) %collective-permute-start.5) | collective-permute-done | bytes 442400 | tf_op jit(solution)/shard_map/ppermute | solution.py:58
  117.2 33.1 %collective-permute-done.36 = bf16[4,96,128]{2,1,0:T(8,128)(2,1)S(1)} collective-permute-done((bf16[4,96,128]{2,1,0:T(8,128)(2,1)S(1)}, bf16[4,96,128]{2,1,0:T(8,128)(2,1)S(1)}, u32[]{:S(2)}, u32[]{:S(2)}) %collective-permute-start.36) | collective-permute-done | bytes 98336 | tf_op jit(solution)/shard_map/ppermute | solution.py:58
  160.8 16.9 %attention_forward.2 = (bf16[1536,192]{1,0:T(8,128)(2,1)}, f32[8,1536]{1,0:T(8,128)}) custom-call(bf16[1536,576]{1,0:T(8,128)(2,1)} %add_convert_fusion.2.query_ref.whole_ref.refs_0_.refs_1_, bf16[1536,576]{1,0:T(8,128)(2,1)} %add_convert_fusion.2.query_ref.whole_ref.refs_0_.refs_1_, s32[1,1536]{1,0:T(1,128)} %broadcast_in_dim.182.row_seg_ref.refs_5_, ...), custom_call_target="tpu_custom_call" | custom-call | flops 7247757312 | bytes 8847360 | tf_op jit(solution)/shard_map/attention_forward/pallas_call | solution.py:255
  188.3 17.1 %attention_forward.3 = (bf16[1536,192]{1,0:T(8,128)(2,1)}, f32[8,1536]{1,0:T(8,128)}) custom-call(bf16[1536,576]{1,0:T(8,128)(2,1)} %add_convert_fusion.1.query_ref.whole_ref.refs_0_.refs_1_, bf16[1536,576]{1,0:T(8,128)(2,1)} %add_convert_fusion.1.query_ref.whole_ref.refs_0_.refs_1_, s32[1,1536]{1,0:T(1,128)} %broadcast_in_dim.184.row_seg_ref.refs_5_, ...), custom_call_target="tpu_custom_call" | custom-call | flops 7247757312 | bytes 8847360 | tf_op jit(solution)/shard_map/attention_forward/pallas_call | solution.py:255
  210.4 4.8 collective-permute-done.16
  229.3 26.8 %multiply_convert_fusion = (bf16[768,3072]{1,0:T(8,128)(2,1)S(1)}, f32[768,3072]{1,0:T(8,128)}, f32[768,3072]{1,0:T(8,128)}) fusion(f32[3072]{0:T(1024)S(1)} %add.601, bf16[768,3072]{1,0:T(8,128)(2,1)S(1)} %bitcast.419, f32[768,768]{1,0:T(8,128)S(1)} %get-tuple-element.362, f32[768]{0:T(1024)S(1)} %add.598, f32[768]{0:T(1024)S(1)} %mul.279, ...), kind=kOutput, calls=%fused_computation.4 | convolution fusion | flops 3782541312 | bytes 30695424 | tf_op jit(solution)/shard_map/dot_general | solution.py:203
  278.9 12.8 %convert_reduce_fusion = (f32[3072]{0:T(1024)S(1)}, bf16[768,3072]{1,0:T(8,128)(2,1)}) fusion(f32[768,3072]{1,0:T(8,128)} %get-tuple-element.236, f32[768,3072]{1,0:T(8,128)} %get-tuple-element.363, f32[3072]{0:T(1024)S(1)} %add.601, bf16[768,768]{1,0:T(8,128)(2,1)S(1)} %get-tuple-element.220, bf16[3072,768]{1,0:T(8,128)(2,1)S(1)} %bitcast.418), kind=kOutput, calls=%fused_computation.2 | convolution fusion | flops 3663983616 | bytes 29515776 | tf_op jit(solution)/shard_map/dot_general | solution.py:211
  291.7 6.9 %multiply_reduce_fusion.1 = (f32[768]{0:T(1024)S(1)}, f32[768]{0:T(1024)S(1)}, f32[768]{0:T(1024)S(1)}, f32[768,768]{1,0:T(8,128)S(1)}) fusion(f32[768,768]{1,0:T(8,128)S(1)} %copy-done.4, f32[768]{0:T(1024)S(1)} %fusion.49, f32[768]{0:T(1024)S(1)} %broadcast_multiply_fusion.1, f32[768]{0:T(1024)S(1)} %mul.279, bf16[768,3072]{1,0:T(8,128)(2,1)} %get-tuple-element.222, ...), kind=kOutput, calls=%fused_computation.46 | convolution fusion | flops 3629774592 | bytes 16536576 | tf_op jit(solution)/shard_map/dot_general | solution.py:211
  303.1 12.5 %fusion.87 = f32[3072,768]{1,0:T(8,128)} fusion(bf16[768,3072]{1,0:T(8,128)(2,1)} %copy-done.78, bf16[768,768]{1,0:T(8,128)(2,1)S(1)} %copy-done.28), kind=kOutput, calls=%fused_computation.399 | convolution fusion | flops 3623878656 | bytes 15335424 | tf_op jit(solution)/shard_map/dot_general | solution.py:207
  368.5 5.1 collective-permute-done.50
  390.0 12.3 %attention_backward.9 = (bf16[512,192]{1,0:T(8,128)(2,1)}, f32[3,1536,64]{2,1,0:T(8,128)}, f32[3,1536,64]{2,1,0:T(8,128)}) custom-call(bf16[1536,576]{1,0:T(8,128)(2,1)} %add_convert_fusion.1.query_ref.whole_ref.refs_0_.refs_1_, bf16[1536,576]{1,0:T(8,128)(2,1)} %add_convert_fusion.1.query_ref.whole_ref.refs_0_.refs_1_, ...), custom_call_target="tpu_custom_call" | custom-call | flops 6039797760 | bytes 12386304 | tf_op jit(solution)/shard_map/attention_backward/pallas_call | solution.py:361
  419.3 12.1 %attention_backward.6 = (bf16[512,192]{1,0:T(8,128)(2,1)}, f32[3,1536,64]{2,1,0:T(8,128)}, f32[3,1536,64]{2,1,0:T(8,128)}) custom-call(bf16[1536,576]{1,0:T(8,128)(2,1)} %add_convert_fusion.2.query_ref.whole_ref.refs_0_.refs_1_, bf16[1536,576]{1,0:T(8,128)(2,1)} %add_convert_fusion.2.query_ref.whole_ref.refs_0_.refs_1_, ...), custom_call_target="tpu_custom_call" | custom-call | flops 6039797760 | bytes 12386304 | tf_op jit(solution)/shard_map/attention_backward/pallas_call | solution.py:361
  431.4 13.9 %attention_backward.7 = (bf16[512,192]{1,0:T(8,128)(2,1)}, f32[3,1536,64]{2,1,0:T(8,128)}, f32[3,1536,64]{2,1,0:T(8,128)}) custom-call(bf16[1536,576]{1,0:T(8,128)(2,1)} %add_convert_fusion.2.query_ref.whole_ref.refs_0_.refs_1_, bf16[1536,576]{1,0:T(8,128)(2,1)} %add_convert_fusion.2.query_ref.whole_ref.refs_0_.refs_1_, ...), custom_call_target="tpu_custom_call" | custom-call | flops 6039797760 | bytes 12386304 | tf_op jit(solution)/shard_map/attention_backward/pallas_call | solution.py:361
  447.2 29.1 %collective-permute-done.45 = bf16[8,192,384]{2,1,0:T(8,128)(2,1)} collective-permute-done((bf16[8,192,384]{2,1,0:T(8,128)(2,1)}, bf16[8,192,384]{2,1,0:T(8,128)(2,1)}, u32[]{:S(2)}, u32[]{:S(2)}) %collective-permute-start.45) | collective-permute-done | bytes 1179680 | tf_op jit(solution)/shard_map/ppermute | solution.py:37
  482.2 12.6 %attention_backward.8 = (bf16[512,192]{1,0:T(8,128)(2,1)}, bf16[1536,192]{1,0:T(8,128)(2,1)}, bf16[1536,192]{1,0:T(8,128)(2,1)}) custom-call(bf16[1536,576]{1,0:T(8,128)(2,1)} %add_convert_fusion.2.query_ref.whole_ref.refs_0_.refs_1_, bf16[1536,576]{1,0:T(8,128)(2,1)} %add_convert_fusion.2.query_ref.whole_ref.refs_0_.refs_1_, ...), custom_call_target="tpu_custom_call" | custom-call | flops 6039797760 | bytes 12386304 | tf_op jit(solution)/shard_map/attention_backward/pallas_call | solution.py:361
  510.8 14.1 %attention_backward.10 = (bf16[512,192]{1,0:T(8,128)(2,1)}, f32[3,1536,64]{2,1,0:T(8,128)}, f32[3,1536,64]{2,1,0:T(8,128)}) custom-call(bf16[1536,576]{1,0:T(8,128)(2,1)} %add_convert_fusion.1.query_ref.whole_ref.refs_0_.refs_1_, bf16[1536,576]{1,0:T(8,128)(2,1)} %add_convert_fusion.1.query_ref.whole_ref.refs_0_.refs_1_, ...), custom_call_target="tpu_custom_call" | custom-call | flops 6039797760 | bytes 12386304 | tf_op jit(solution)/shard_map/attention_backward/pallas_call | solution.py:361
  532.1 12.8 %attention_backward.11 = (bf16[512,192]{1,0:T(8,128)(2,1)}, bf16[1536,192]{1,0:T(8,128)(2,1)}, bf16[1536,192]{1,0:T(8,128)(2,1)}) custom-call(bf16[1536,576]{1,0:T(8,128)(2,1)} %add_convert_fusion.1.query_ref.whole_ref.refs_0_.refs_1_, bf16[1536,576]{1,0:T(8,128)(2,1)} %add_convert_fusion.1.query_ref.whole_ref.refs_0_.refs_1_, ...), custom_call_target="tpu_custom_call" | custom-call | flops 6039797760 | bytes 12386304 | tf_op jit(solution)/shard_map/attention_backward/pallas_call | solution.py:361
  547.3 4.8 fusion.72
  557.8 5.6 convolution_add_fusion
  617.6 5.3 collective-permute-done.62
  644.8 6.5 collective-permute-done.59
  (680 shorter events, 345.3 us)
Async XLA Ops:
  3.0 42.8 %collective-permute-start.2 = (bf16[1,96,576]{1,2,0:T(8,128)(2,1)S(1)}, bf16[1,96,576]{1,2,0:T(8,128)(2,1)}, u32[]{:S(2)}, u32[]{:S(2)}) collective-permute-start(bf16[1,96,576]{1,2,0:T(8,128)(2,1)S(1)} %bitcast.447), channel_id=1, source_target_pairs={{0,2},{1,3},{2,4},{3,5},{4,6},{5,7},{6,0},{7,1},{8,10},{9,11},{10,... | collective-permute-start | bytes 331784 | tf_op jit(solution)/shard_map/ppermute | solution.py:58
  4.6 43.1 %collective-permute-start.3 = (bf16[1,96,576]{1,2,0:T(8,128)(2,1)S(1)}, bf16[1,96,576]{1,2,0:T(8,128)(2,1)}, u32[]{:S(2)}, u32[]{:S(2)}) collective-permute-start(bf16[1,96,576]{1,2,0:T(8,128)(2,1)S(1)} %bitcast.448), channel_id=1, source_target_pairs={{0,4},{1,5},{2,6},{3,7},{4,0},{5,1},{6,2},{7,3},{8,12},{9,13},{10,... | collective-permute-start | bytes 331784 | tf_op jit(solution)/shard_map/ppermute | solution.py:58
  19.8 30.9 %collective-permute-start.4 = (bf16[1,96,576]{1,2,0:T(8,128)(2,1)S(1)}, bf16[1,96,576]{1,2,0:T(8,128)(2,1)}, u32[]{:S(2)}, u32[]{:S(2)}) collective-permute-start(bf16[1,96,576]{1,2,0:T(8,128)(2,1)S(1)} %bitcast.450), channel_id=1, source_target_pairs={{0,6},{1,7},{2,0},{3,1},{4,2},{5,3},{6,4},{7,5},{8,14},{9,15},{10,... | collective-permute-start | bytes 331784 | tf_op jit(solution)/shard_map/ppermute | solution.py:58
  45.8 31.4 %collective-permute-start.30 = (bf16[1,192,768]{2,1,0:T(8,128)(2,1)}, bf16[1,192,768]{2,1,0:T(8,128)(2,1)}, u32[]{:S(2)}, u32[]{:S(2)}) collective-permute-start(bf16[1,192,768]{2,1,0:T(8,128)(2,1)} %get-tuple-element.234), channel_id=1, source_target_pairs={{0,6},{1,7},{2,0},{3,1},{4,2},{5,3},{6,4},{7,5},{8,14},{9,15},{10,... | collective-permute-start | bytes 884744 | tf_op jit(solution)/shard_map/ppermute | solution.py:58
  47.7 33.3 %collective-permute-start.23 = (bf16[1,48,3072]{2,1,0:T(8,128)(2,1)}, bf16[1,48,3072]{2,1,0:T(8,128)(2,1)}, u32[]{:S(2)}, u32[]{:S(2)}) collective-permute-start(bf16[1,48,3072]{2,1,0:T(8,128)(2,1)} %get-tuple-element.238), channel_id=1, source_target_pairs={{0,2},{1,3},{2,4},{3,5},{4,6},{5,7},{6,0},{7,1},{8,10},{9,11},{10,... | collective-permute-start | bytes 884744 | tf_op jit(solution)/shard_map/ppermute | solution.py:58
  50.6 33.6 %collective-permute-start.24 = (bf16[1,48,3072]{2,1,0:T(8,128)(2,1)}, bf16[1,48,3072]{2,1,0:T(8,128)(2,1)}, u32[]{:S(2)}, u32[]{:S(2)}) collective-permute-start(bf16[1,48,3072]{2,1,0:T(8,128)(2,1)} %get-tuple-element.238), channel_id=1, source_target_pairs={{0,4},{1,5},{2,6},{3,7},{4,0},{5,1},{6,2},{7,3},{8,12},{9,13},{10,... | collective-permute-start | bytes 884744 | tf_op jit(solution)/shard_map/ppermute | solution.py:58
  57.4 29.0 %collective-permute-start.25 = (bf16[1,48,3072]{2,1,0:T(8,128)(2,1)}, bf16[1,48,3072]{2,1,0:T(8,128)(2,1)S(1)}, u32[]{:S(2)}, u32[]{:S(2)}) collective-permute-start(bf16[1,48,3072]{2,1,0:T(8,128)(2,1)} %get-tuple-element.238), channel_id=1, source_target_pairs={{0,6},{1,7},{2,0},{3,1},{4,2},{5,3},{6,4},{7,5},{8,14},{9,15},{10,... | collective-permute-start | bytes 884744 | tf_op jit(solution)/shard_map/ppermute | solution.py:58
  74.7 40.1 %collective-permute-start = (bf16[384,768]{1,0:T(8,128)(2,1)}, bf16[384,768]{1,0:T(8,128)(2,1)S(1)}, u32[]{:S(2)}, u32[]{:S(2)}) collective-permute-start(bf16[384,768]{1,0:T(8,128)(2,1)} %get-tuple-element.285), channel_id=1, source_target_pairs={{0,16},{8,24},{16,0},{24,8},{1,17},{9,25},{17,1},{25,9},{2,18},{10... | collective-permute-start | bytes 1769480 | tf_op jit(solution)/shard_map/ppermute | solution.py:37
  77.2 38.2 %collective-permute-start.13 = (bf16[384,768]{1,0:T(8,128)(2,1)}, bf16[384,768]{1,0:T(8,128)(2,1)S(1)}, u32[]{:S(2)}, u32[]{:S(2)}) collective-permute-start(bf16[384,768]{1,0:T(8,128)(2,1)} %get-tuple-element.286), channel_id=1, source_target_pairs={{0,16},{8,24},{16,0},{24,8},{1,17},{9,25},{17,1},{25,9},{2,18},{10... | collective-permute-start | bytes 1769480 | tf_op jit(solution)/shard_map/ppermute | solution.py:37
  86.4 65.1 %collective-permute-start.31 = (bf16[4,192,768]{2,1,0:T(8,128)(2,1)S(1)}, bf16[4,192,768]{2,1,0:T(8,128)(2,1)S(1)}, u32[]{:S(2)}, u32[]{:S(2)}) collective-permute-start(bf16[4,192,768]{2,1,0:T(8,128)(2,1)S(1)} %constant_dynamic-update-slice_fusion.4), channel_id=1, source_target_pairs={{0,1},{1,0},{2,3},{3,2},{4,5},{5,4},{6,7},{7,6},{8,9},{9,8},{10,11... | collective-permute-start | bytes 3538952 | tf_op jit(solution)/shard_map/ppermute | solution.py:58
  90.9 61.6 %collective-permute-start.26 = (bf16[4,48,3072]{2,1,0:T(8,128)(2,1)}, bf16[4,48,3072]{2,1,0:T(8,128)(2,1)S(1)}, u32[]{:S(2)}, u32[]{:S(2)}) collective-permute-start(bf16[4,48,3072]{2,1,0:T(8,128)(2,1)} %constant_dynamic-update-slice_fusion.8), channel_id=1, source_target_pairs={{0,1},{1,0},{2,3},{3,2},{4,5},{5,4},{6,7},{7,6},{8,9},{9,8},{10,11... | collective-permute-start | bytes 3538952 | tf_op jit(solution)/shard_map/ppermute | solution.py:58
  114.7 35.6 %collective-permute-start.22 = (bf16[8,48,768]{2,1,0:T(8,128)(2,1)S(1)}, bf16[8,48,768]{2,1,0:T(8,128)(2,1)S(1)}, u32[]{:S(2)}, u32[]{:S(2)}) collective-permute-start(bf16[8,48,768]{2,1,0:T(8,128)(2,1)S(1)} %bitcast.428), channel_id=1, source_target_pairs={{0,8},{8,0},{16,24},{24,16},{1,9},{9,1},{17,25},{25,17},{2,10},{10... | collective-permute-start | bytes 1769480 | tf_op jit(solution)/shard_map/ppermute | solution.py:37
  114.7 35.5 %collective-permute-start.36 = (bf16[4,96,128]{2,1,0:T(8,128)(2,1)S(1)}, bf16[4,96,128]{2,1,0:T(8,128)(2,1)S(1)}, u32[]{:S(2)}, u32[]{:S(2)}) collective-permute-start(bf16[4,96,128]{2,1,0:T(8,128)(2,1)S(1)} %constant_dynamic-update-slice_fusion), channel_id=1, source_target_pairs={{0,1},{1,0},{2,3},{3,2},{4,5},{5,4},{6,7},{7,6},{8,9},{9,8},{10,11... | collective-permute-start | bytes 294920 | tf_op jit(solution)/shard_map/ppermute | solution.py:58
  115.7 39.9 %collective-permute-start.1 = (bf16[2,384,768]{2,1,0:T(8,128)(2,1)S(1)}, bf16[2,384,768]{2,1,0:T(8,128)(2,1)S(1)}, u32[]{:S(2)}, u32[]{:S(2)}) collective-permute-start(bf16[2,384,768]{2,1,0:T(8,128)(2,1)S(1)} %pad_maximum_fusion.9), channel_id=1, source_target_pairs={{0,8},{8,0},{16,24},{24,16},{1,9},{9,1},{17,25},{25,17},{2,10},{10... | collective-permute-start | bytes 3538952 | tf_op jit(solution)/shard_map/ppermute | solution.py:37
  150.3 31.4 %collective-permute-start.14 = (bf16[2,384,768]{2,1,0:T(8,128)(2,1)}, bf16[2,384,768]{2,1,0:T(8,128)(2,1)}, u32[]{:S(2)}, u32[]{:S(2)}) collective-permute-start(bf16[2,384,768]{2,1,0:T(8,128)(2,1)} %pad_maximum_fusion.10), channel_id=1, source_target_pairs={{0,8},{8,0},{16,24},{24,16},{1,9},{9,1},{17,25},{25,17},{2,10},{10... | collective-permute-start | bytes 3538952 | tf_op jit(solution)/shard_map/ppermute | solution.py:37
  151.9 68.8 %collective-permute-start.32 = (bf16[8,192,768]{2,1,0:T(8,128)(2,1)S(1)}, bf16[8,192,768]{2,1,0:T(8,128)(2,1)}, u32[]{:S(2)}, u32[]{:S(2)}) collective-permute-start(bf16[8,192,768]{2,1,0:T(8,128)(2,1)S(1)} %bitcast.401), channel_id=1, source_target_pairs={{0,8},{8,0},{16,24},{24,16},{1,9},{9,1},{17,25},{25,17},{2,10},{10... | collective-permute-start | bytes 7077896 | tf_op jit(solution)/shard_map/ppermute | solution.py:37
  155.7 68.3 %collective-permute-start.27 = (bf16[8,48,3072]{2,1,0:T(8,128)(2,1)}, bf16[8,48,3072]{2,1,0:T(8,128)(2,1)}, u32[]{:S(2)}, u32[]{:S(2)}) collective-permute-start(bf16[8,48,3072]{2,1,0:T(8,128)(2,1)} %bitcast.62), channel_id=1, source_target_pairs={{0,8},{8,0},{16,24},{24,16},{1,9},{9,1},{17,25},{25,17},{2,10},{10... | collective-permute-start | bytes 7077896 | tf_op jit(solution)/shard_map/ppermute | solution.py:37
  324.4 80.8 %collective-permute-start.44 = (bf16[8,48,768]{2,1,0:T(8,128)(2,1)}, bf16[8,48,768]{2,1,0:T(8,128)(2,1)}, u32[]{:S(2)}, u32[]{:S(2)}) collective-permute-start(bf16[8,48,768]{2,1,0:T(8,128)(2,1)} %fusion.19), channel_id=1, source_target_pairs={{0,8},{8,0},{16,24},{24,16},{1,9},{9,1},{17,25},{25,17},{2,10},{10... | collective-permute-start | bytes 1769480 | tf_op jit(solution)/shard_map/ppermute | solution.py:37
  326.7 79.8 %collective-permute-start.43 = (bf16[8,48,3072]{2,1,0:T(8,128)(2,1)}, bf16[8,48,3072]{2,1,0:T(8,128)(2,1)}, u32[]{:S(2)}, u32[]{:S(2)}) collective-permute-start(bf16[8,48,3072]{2,1,0:T(8,128)(2,1)} %fusion.6), channel_id=1, source_target_pairs={{0,8},{8,0},{16,24},{24,16},{1,9},{9,1},{17,25},{25,17},{2,10},{10... | collective-permute-start | bytes 7077896 | tf_op jit(solution)/shard_map/ppermute | solution.py:37
  416.2 29.1 %collective-permute-start.57 = (bf16[8,48,384]{2,1,0:T(8,128)(2,1)S(1)}, bf16[8,48,384]{2,1,0:T(8,128)(2,1)}, u32[]{:S(2)}, u32[]{:S(2)}) collective-permute-start(bf16[8,48,384]{2,1,0:T(8,128)(2,1)S(1)} %select_convert_fusion.2), channel_id=1, source_target_pairs={{0,16},{8,24},{16,0},{24,8},{1,17},{9,25},{17,1},{25,9},{2,18},{10... | collective-permute-start | bytes 884744 | tf_op jit(solution)/shard_map/ppermute | solution.py:37
  417.2 85.4 %collective-permute-start.52 = (bf16[8,48,1536]{2,1,0:T(8,128)(2,1)}, bf16[8,48,1536]{2,1,0:T(8,128)(2,1)}, u32[]{:S(2)}, u32[]{:S(2)}) collective-permute-start(bf16[8,48,1536]{2,1,0:T(8,128)(2,1)} %select_convert_fusion), channel_id=1, source_target_pairs={{0,16},{8,24},{16,0},{24,8},{1,17},{9,25},{17,1},{25,9},{2,18},{10... | collective-permute-start | bytes 3538952 | tf_op jit(solution)/shard_map/ppermute | solution.py:37
  418.2 58.0 %collective-permute-start.45 = (bf16[8,192,384]{2,1,0:T(8,128)(2,1)}, bf16[8,192,384]{2,1,0:T(8,128)(2,1)}, u32[]{:S(2)}, u32[]{:S(2)}) collective-permute-start(bf16[8,192,384]{2,1,0:T(8,128)(2,1)} %select_convert_fusion.1), channel_id=1, source_target_pairs={{0,16},{8,24},{16,0},{24,8},{1,17},{9,25},{17,1},{25,9},{2,18},{10... | collective-permute-start | bytes 3538952 | tf_op jit(solution)/shard_map/ppermute | solution.py:37
  529.8 115.0 %collective-permute-start.47 = (bf16[384,768]{1,0:T(8,128)(2,1)}, bf16[384,768]{1,0:T(8,128)(2,1)}, u32[]{:S(2)}, u32[]{:S(2)}) collective-permute-start(bf16[384,768]{1,0:T(8,128)(2,1)} %fusion.20), channel_id=1, source_target_pairs={{0,16},{8,24},{16,0},{24,8},{1,17},{9,25},{17,1},{25,9},{2,18},{10... | collective-permute-start | bytes 1769480 | tf_op jit(solution)/shard_map/ppermute | solution.py:37
  556.4 34.0 %collective-permute-start.89 = (bf16[192,384]{1,0:T(8,128)(2,1)S(1)}, bf16[192,384]{1,0:T(8,128)(2,1)S(1)}, u32[]{:S(2)}, u32[]{:S(2)}) collective-permute-start(bf16[192,384]{1,0:T(8,128)(2,1)S(1)} %add_bitcast_fusion), channel_id=1, source_target_pairs={{0,16},{8,24},{16,0},{24,8},{1,17},{9,25},{17,1},{25,9},{2,18},{10... | collective-permute-start | bytes 442376 | tf_op jit(solution)/shard_map/ppermute | solution.py:37
  (159 other events, 1798.0 us)
